TPU v7x, 32 devices: a whole 2x2x4 slice. The times are simulated.
32 devices in a mesh: dp: 16 (over z, y, x), tensor: 2 (over core).
Axes of the slice: x: 2, y: 2, z: 4, core: 2. Of those that a mesh axis runs over, the one named last changes fastest.
Arguments:
- tokens: bfloat16 [2048, 8192], P('dp', 'tensor'), may hold values from -6 to 6
- gate_left: bfloat16 [8192, 1024], P(None, 'tensor'), may hold values from -0.0625 to 0.0625
- gate_right: bfloat16 [1024, 14336], P(None, 'tensor'), may hold values from -0.1875 to 0.1875
- up_left: bfloat16 [8192, 1024], P(None, 'tensor'), may hold values from -0.0625 to 0.0625
- up_right: bfloat16 [1024, 14336], P(None, 'tensor'), may hold values from -0.1875 to 0.1875
- hidden_grad: bfloat16 [2048, 14336], P('dp', 'tensor'), may hold values from -6 to 6
Outputs:
- input_grad: bfloat16 [2048, 8192], P('dp', 'tensor')
- gate_left_grad: bfloat16 [8192, 1024], P('dp', 'tensor')
- gate_right_grad: bfloat16 [1024, 14336], P('dp', 'tensor')
- up_left_grad: bfloat16 [8192, 1024], P('dp', 'tensor')
- up_right_grad: bfloat16 [1024, 14336], P('dp', 'tensor')
All inputs are finite; a program needn't handle non-finite values.
Results may differ from a plain program's by a relative error of at most 0.02.
Values may be sent and summed in bfloat16 or wider, within the bound.
No kernel may reach another device: no remote copies, remote signals or barrier semaphores. Data moves between devices by JAX's collectives and lax.ppermute only.
A program may use at most 256 MiB of HBM per device.

v0:
```python
import jax
import jax.numpy as jnp
from jax import lax
from jax.sharding import PartitionSpec as P


def product(left, right, left_dim, right_dim):
    return lax.dot_general(
        left, right, (((left_dim,), (right_dim,)), ((), ())), preferred_element_type=jnp.float32
    )


def body(tokens, gate_left, gate_right, up_left, up_right, hidden_grad):
    groups = lax.axis_size("dp")
    loss_scale = float(tokens.shape[0] * groups) ** (-0.5)
    gathered = lax.all_gather(tokens, "tensor", axis=1, tiled=True)
    gate_part = product(gathered, gate_left, 1, 0).astype(jnp.bfloat16)
    up_part = product(gathered, up_left, 1, 0).astype(jnp.bfloat16)
    gate_codes, up_codes = (
        lax.all_gather(gate_part, "tensor", axis=1, tiled=True),
        lax.all_gather(up_part, "tensor", axis=1, tiled=True),
    )
    gate_pre = product(gate_codes, gate_right, 1, 0)
    up_pre = product(up_codes, up_right, 1, 0)
    sigmoid_gate = jax.nn.sigmoid(gate_pre)
    upstream = hidden_grad.astype(jnp.float32)
    up_delta = (upstream * gate_pre * sigmoid_gate).astype(jnp.bfloat16)
    gate_delta = (
        upstream * up_pre * sigmoid_gate * (1.0 + gate_pre * (1.0 - sigmoid_gate))
    ).astype(jnp.bfloat16)
    gate_sum, up_sum = (
        lax.psum_scatter(
            product(gate_delta, gate_right, 1, 1).astype(jnp.bfloat16),
            "tensor",
            scatter_dimension=1,
            tiled=True,
        ).astype(jnp.float32),
        lax.psum_scatter(
            product(up_delta, up_right, 1, 1).astype(jnp.bfloat16),
            "tensor",
            scatter_dimension=1,
            tiled=True,
        ).astype(jnp.float32),
    )
    gate_rank = gate_sum.astype(jnp.bfloat16)
    up_rank = up_sum.astype(jnp.bfloat16)
    input_terms = product(gate_rank, gate_left, 1, 1) + product(up_rank, up_left, 1, 1)
    input_grad = lax.psum_scatter(
        input_terms.astype(jnp.bfloat16), "tensor", scatter_dimension=1, tiled=True
    )
    gate_term = (product(gate_codes, gate_delta, 0, 0) * loss_scale).astype(jnp.bfloat16)
    up_term = (product(up_codes, up_delta, 0, 0) * loss_scale).astype(jnp.bfloat16)
    gate_right_sum, up_right_sum = (
        lax.psum_scatter(gate_term, "dp", scatter_dimension=0, tiled=True).astype(jnp.float32),
        lax.psum_scatter(up_term, "dp", scatter_dimension=0, tiled=True).astype(jnp.float32),
    )
    gate_left_sum, up_left_sum = (
        lax.psum_scatter(
            (product(gathered, gate_rank, 0, 0) * loss_scale).astype(jnp.bfloat16),
            "dp",
            scatter_dimension=0,
            tiled=True,
        ).astype(jnp.float32),
        lax.psum_scatter(
            (product(gathered, up_rank, 0, 0) * loss_scale).astype(jnp.bfloat16),
            "dp",
            scatter_dimension=0,
            tiled=True,
        ).astype(jnp.float32),
    )
    return (
        input_grad,
        gate_left_sum.astype(jnp.bfloat16),
        gate_right_sum.astype(jnp.bfloat16),
        up_left_sum.astype(jnp.bfloat16),
        up_right_sum.astype(jnp.bfloat16),
    )


def solution(mesh):
    placed = (
        P("dp", "tensor"),
        P(None, "tensor"),
        P(None, "tensor"),
        P(None, "tensor"),
        P(None, "tensor"),
        P("dp", "tensor"),
    )
    return jax.shard_map(
        body,
        mesh=mesh,
        in_specs=placed,
        out_specs=(
            P("dp", "tensor"),
            P("dp", "tensor"),
            P("dp", "tensor"),
            P("dp", "tensor"),
            P("dp", "tensor"),
        ),
        check_vma=False,
    )
```

profile of v0, /device:TPU:10, one launch (start us, length us, event | category | flops | bytes accessed | tf_op | source)
XLA Modules:
  0.0 1095.3 jit_solution(15033348859214570247)
XLA Ops:
  7.2 0.7 all-gather.2.cloned.1.call-update
  7.9 13.6 %all-gather.2.cloned.1.call-done = bf16[128,8192]{1,0:T(8,128)(2,1)} async-done(((bf16[128,4096]{1,0:T(8,128)(2,1)}), bf16[128,8192]{1,0:T(8,128)(2,1)}) %all-gather.2.cloned.1.call-update) | async-done | bytes 2097168 | tf_op jit(solution)/shard_map/all_gather | solution.py:16
  21.5 5.4 convolution_convert_fusion.2
  27.0 2.1 all_gather.11
  29.1 4.8 convolution_convert_fusion.3
  33.9 2.0 all_gather.10
  35.9 3.9 fusion.10
  39.9 12.5 %convolution_convert_fusion = bf16[128,1024]{1,0:T(8,128)(2,1)} fusion(bf16[1024,7168]{1,0:T(8,128)(2,1)} %param.10, f32[128,7168]{1,0:T(8,128)} %fusion.10, bf16[128,7168]{1,0:T(8,128)(2,1)} %param.11), kind=kOutput, calls=%fused_computation.16 | convolution fusion | flops 1885601792 | bytes 20447232 | tf_op jit(solution)/shard_map/dot_general | solution.py:8
  52.4 0.2 reduce-scatter.8.cloned.1.call-start
  52.6 10.5 fusion.5
  63.1 1.2 copy-done.1
  64.4 10.8 convolution_convert_fusion.1
  75.2 0.0 reduce-scatter.18.cloned.1.call-start
  75.3 6.5 fusion.1
  81.7 0.0 reduce-scatter.14.cloned.1.call-start
  81.8 2.4 reduce-scatter.8.cloned.1.call-done
  84.2 6.6 fusion
  90.9 0.3 reduce-scatter.12.cloned.1.call-start
  91.1 0.6 copy-done.4
  91.7 6.6 fusion.11
  98.4 7.7 fusion.2
  106.1 0.0 reduce-scatter.20.cloned.1.call-start
  106.2 9.5 multiply_convert_fusion
  115.8 1.5 copy-done.2
  117.2 7.3 multiply_convert_fusion.1
  124.6 143.7 %reduce-scatter.18.cloned.1.call-done = bf16[512,512]{0,1:T(8,128)(2,1)} async-done(((bf16[8192,512]{0,1:T(8,128)(2,1)}), bf16[512,512]{0,1:T(8,128)(2,1)}) %reduce-scatter.18.cloned.1.call-update) | async-done | bytes 524304 | tf_op jit(solution)/shard_map/reduce_scatter | solution.py:64
  268.3 2.0 copy.12
  270.3 180.4 %reduce-scatter.14.cloned.1.call-done = bf16[512,512]{0,1:T(8,128)(2,1)} async-done(((bf16[8192,512]{0,1:T(8,128)(2,1)}), bf16[512,512]{0,1:T(8,128)(2,1)}) %reduce-scatter.14.cloned.1.call-update) | async-done | bytes 524304 | tf_op jit(solution)/shard_map/reduce_scatter | solution.py:58
  450.8 2.0 copy.11
  452.8 10.0 reduce-scatter.12.cloned.1.call-done
  462.8 313.3 %reduce-scatter.20.cloned.1.call-done = bf16[64,7168]{1,0:T(8,128)(2,1)} async-done(((bf16[1024,7168]{1,0:T(8,128)(2,1)}), bf16[64,7168]{1,0:T(8,128)(2,1)}) %reduce-scatter.20.cloned.1.call-update) | async-done | bytes 917520 | tf_op jit(solution)/shard_map/reduce_scatter | solution.py:55
  776.1 312.4 %reduce-scatter.16.cloned.1.call-done = bf16[64,7168]{1,0:T(8,128)(2,1)} async-done(((bf16[1024,7168]{1,0:T(8,128)(2,1)}), bf16[64,7168]{1,0:T(8,128)(2,1)}) %reduce-scatter.16.cloned.1.call-update) | async-done | bytes 917520 | tf_op jit(solution)/shard_map/reduce_scatter | solution.py:54
  (29 shorter events, 0.3 us)
Async XLA Ops:
  7.2 14.4 %all-gather.2.cloned.1.call-start = ((), (), s32[]{:S(2)}) async-start(), calls=%async_computation.7 | async-start | bytes 3145728 | tf_op jit(solution)/shard_map/all_gather | solution.py:16
  7.9 67.4 %reduce-scatter.10.cloned.1.call-start = ((), (), s32[]{:S(2)}) async-start(), calls=%async_computation.9 | async-start | bytes 393216 | tf_op jit(solution)/shard_map/reduce_scatter | solution.py:38
  21.5 7.6 copy-start
  21.5 14.4 %slice-start = ((s8[14680064]{0:T(1024)(128)(4,1)}), s8[4194304]{0:T(1024)(128)(4,1)S(1)}, s32[]{:S(2)}) async-start(s8[14680064]{0:T(1024)(128)(4,1)} %bitcast.26), calls=%async_computation.15 | async-start | bytes 8388608
  21.5 14.4 %slice-start.1 = ((s8[14680064]{0:T(1024)(128)(4,1)}), s8[4194304]{0:T(1024)(128)(4,1)S(1)}, s32[]{:S(2)}) async-start(s8[14680064]{0:T(1024)(128)(4,1)} %bitcast.26), calls=%async_computation.16 | async-start | bytes 8388608
  27.0 8.9 slice-start.2
  29.1 6.8 slice-start.3
  52.4 31.9 %reduce-scatter.8.cloned.1.call-start = ((), (), s32[]{:S(2)}) async-start(), calls=%async_computation.8 | async-start | bytes 393216 | tf_op jit(solution)/shard_map/reduce_scatter | solution.py:32
  63.1 1.2 copy-start.1
  75.2 193.1 %reduce-scatter.18.cloned.1.call-start = ((), (), s32[]{:S(2)}) async-start(), calls=%async_computation.13 | async-start | bytes 8912896 | tf_op jit(solution)/shard_map/reduce_scatter | solution.py:64
  81.7 369.0 %reduce-scatter.14.cloned.1.call-start = ((), (), s32[]{:S(2)}) async-start(), calls=%async_computation.11 | async-start | bytes 8912896 | tf_op jit(solution)/shard_map/reduce_scatter | solution.py:58
  90.8 0.9 copy-start.4
  90.8 7.5 copy-start.3
  90.9 371.9 %reduce-scatter.12.cloned.1.call-start = ((), (), s32[]{:S(2)}) async-start(), calls=%async_computation.10 | async-start | bytes 3145728 | tf_op jit(solution)/shard_map/reduce_scatter | solution.py:48
  98.4 7.8 copy-start.5
  106.1 670.0 %reduce-scatter.20.cloned.1.call-start = ((), (), s32[]{:S(2)}) async-start(), calls=%async_computation.14 | async-start | bytes 15597568 | tf_op jit(solution)/shard_map/reduce_scatter | solution.py:55
  115.7 1.5 copy-start.2
  115.7 972.8 %reduce-scatter.16.cloned.1.call-start = ((), (), s32[]{:S(2)}) async-start(), calls=%async_computation.12 | async-start | bytes 15597568 | tf_op jit(solution)/shard_map/reduce_scatter | solution.py:54
Sparse Core Ops, SparseCore 0:
  9.5 11.9 all-gather.1
  52.5 8.8 reduce-scatter.9
  75.3 8.8 reduce-scatter.7
  86.4 181.8 reduce-scatter.17
  270.4 180.2 reduce-scatter.13
  453.4 9.3 reduce-scatter.11
  465.7 310.3 reduce-scatter.19
  779.0 309.4 reduce-scatter.15
where the time goes:
time: 1100 us
  waiting for transfers between devices  977 us (89%)
  matrix products  92.2 us (8%)
  between operations  14.2 us (1%)
    reduce_scatter x1, waiting for transfers between devices, body(): lax.psum_scatter(up_term, 'dp', scatter_dimension=0, tiled=True)  313 us
    reduce_scatter x1, waiting for transfers between devices, body(): lax.psum_scatter(gate_term, 'dp', scatter_dimension=0, tiled=True)  312 us
    reduce_scatter x1, waiting for transfers between devices, body(): lax.psum_scatter((product(gathered, gate_rank, 0, 0) * loss_scale).astype...  180 us
    reduce_scatter x1, waiting for transfers between devices, body(): lax.psum_scatter((product(gathered, up_rank, 0, 0) * loss_scale).astype(j...  144 us
    dot_general x12, matrix products, product(): lax.dot_general(left, right, (((left_dim,), (right_dim,)), ((), ())), pre...  92.2 us
  transfers between devices with their start and end apart: 8, of which 7 were waited for; matrix products, arithmetic and copies ran while one was open for 6% of the time, Pallas kernels for 0%

commit v1 on v0

v1 whole, which is shorter than its diff:
```python
import jax
import jax.numpy as jnp
from jax import lax
from jax.sharding import PartitionSpec as P


def product(left, right, left_dim, right_dim):
    return lax.dot_general(
        left, right, (((left_dim,), (right_dim,)), ((), ())), preferred_element_type=jnp.float32
    )


def join(values, axis):
    if lax.axis_size("tensor") != 2:
        return lax.all_gather(values, "tensor", axis=axis, tiled=True)
    other = lax.ppermute(values, "tensor", [(0, 1), (1, 0)])
    first = lax.axis_index("tensor") == 0
    return jnp.where(
        first,
        jnp.concatenate([values, other], axis),
        jnp.concatenate([other, values], axis),
    )


def total(values):
    axis = values.ndim - 1
    if lax.axis_size("tensor") != 2:
        return lax.psum_scatter(values, "tensor", scatter_dimension=axis, tiled=True)
    half = values.shape[-1] // 2
    low, high = values[..., :half], values[..., half:]
    first = lax.axis_index("tensor") == 0
    other = lax.ppermute(jnp.where(first, high, low), "tensor", [(0, 1), (1, 0)])
    kept = jnp.where(first, low, high)
    return (kept.astype(jnp.float32) + other.astype(jnp.float32)).astype(values.dtype)


def exchange(values):
    return lax.all_to_all(values, "dp", split_axis=0, concat_axis=0, tiled=True)


def spread(first, second):
    n = lax.axis_size("dp")
    lines = 4
    plane = n // lines
    both = jnp.stack([first, second])
    groups = [[a * plane + b for a in range(lines)] for b in range(plane)]
    line = lax.all_to_all(
        jnp.broadcast_to(both[None], (lines,) + both.shape),
        "dp",
        split_axis=0,
        concat_axis=0,
        tiled=True,
        axis_index_groups=groups,
    )
    bits = [1 << i for i in range(plane.bit_length() - 1)]
    here = lax.axis_index("dp") % plane
    out = []
    for which, order in ((0, bits), (1, bits[::-1])):
        held = line[:, which][None]
        offsets = [0]
        for bit in order:
            came = lax.ppermute(held, "dp", [(i, i ^ bit) for i in range(n)])
            held = jnp.concatenate([held, came])
            offsets = offsets + [o ^ bit for o in offsets]
        place = jnp.asarray([offsets.index(o) for o in range(plane)])
        blocks = [
            lax.dynamic_index_in_dim(held, place[here ^ b], 0, keepdims=False)
            for b in range(plane)
        ]
        out.append(jnp.stack(blocks, 1).reshape((n,) + first.shape))
    return out


def deltas(gate_pre, up_pre, upstream):
    gate_sig = jax.nn.sigmoid(gate_pre)
    up_delta = (upstream * gate_pre * gate_sig).astype(jnp.bfloat16)
    gate_delta = (
        upstream * up_pre * gate_sig * (1.0 + gate_pre * (1.0 - gate_sig))
    ).astype(jnp.bfloat16)
    return gate_delta, up_delta


def body(tokens, gate_left, gate_right, up_left, up_right, hidden_grad):
    n, cores = lax.axis_size("dp"), lax.axis_size("tensor")
    here, core = lax.axis_index("dp"), lax.axis_index("tensor")
    rows, units = hidden_grad.shape
    rank = gate_right.shape[0]
    loss_scale = float(rows * n) ** (-0.5)

    share = units // n
    hidden_all = exchange(hidden_grad.reshape(rows, n, share).transpose(1, 0, 2))
    hidden_all = hidden_all.reshape(rows * n, share)

    gathered = join(tokens, 1)
    features = gathered.shape[1]
    mine = gathered.reshape(rows, n, cores, features // n // cores)
    mine = lax.dynamic_index_in_dim(mine, core, 2, keepdims=False).transpose(1, 0, 2)

    gate_part = product(gathered, gate_left, 1, 0).astype(jnp.bfloat16)
    up_part = product(gathered, up_left, 1, 0).astype(jnp.bfloat16)
    gate_codes, up_codes = join(gate_part, 1), join(up_part, 1)
    gate_every, up_every = spread(gate_part, up_part)

    gate_delta, up_delta = deltas(
        product(gate_codes, gate_right, 1, 0),
        product(up_codes, up_right, 1, 0),
        hidden_grad.astype(jnp.float32),
    )
    gate_rank = total(product(gate_delta, gate_right, 1, 1).astype(jnp.bfloat16))
    up_rank = total(product(up_delta, up_right, 1, 1).astype(jnp.bfloat16))
    input_terms = product(gate_rank, gate_left, 1, 1) + product(up_rank, up_left, 1, 1)
    input_grad = total(input_terms.astype(jnp.bfloat16))

    tokens_all = join(exchange(mine), 2).reshape(rows * n, features // n)
    gate_rank_all, up_rank_all = spread(gate_rank, up_rank)
    gate_left_grad = product(tokens_all, gate_rank_all.reshape(rows * n, -1), 0, 0) * loss_scale
    up_left_grad = product(tokens_all, up_rank_all.reshape(rows * n, -1), 0, 0) * loss_scale

    gate_every = join(gate_every, 2).reshape(rows * n, rank)
    up_every = join(up_every, 2).reshape(rows * n, rank)
    gate_slice = lax.dynamic_slice_in_dim(gate_right, here * share, share, 1)
    up_slice = lax.dynamic_slice_in_dim(up_right, here * share, share, 1)
    gate_delta, up_delta = deltas(
        product(gate_every, gate_slice, 1, 0),
        product(up_every, up_slice, 1, 0),
        hidden_all.astype(jnp.float32),
    )
    gate_grad = (product(gate_every, gate_delta, 0, 0) * loss_scale).astype(jnp.bfloat16)
    up_grad = (product(up_every, up_delta, 0, 0) * loss_scale).astype(jnp.bfloat16)
    gate_grad = exchange(gate_grad.reshape(n, rank // n, share))
    up_grad = exchange(up_grad.reshape(n, rank // n, share))

    return (
        input_grad,
        gate_left_grad.astype(jnp.bfloat16),
        gate_grad.transpose(1, 0, 2).reshape(rank // n, units),
        up_left_grad.astype(jnp.bfloat16),
        up_grad.transpose(1, 0, 2).reshape(rank // n, units),
    )


def solution(mesh):
    placed = (
        P("dp", "tensor"),
        P(None, "tensor"),
        P(None, "tensor"),
        P(None, "tensor"),
        P(None, "tensor"),
        P("dp", "tensor"),
    )
    return jax.shard_map(
        body,
        mesh=mesh,
        in_specs=placed,
        out_specs=(P("dp", "tensor"),) * 5,
        check_vma=False,
    )
```

time: 1100 us -> 288 us (0.26)
  waiting for transfers between devices: 977 us -> 85.9 us
  starting transfers between devices: 0.73 us -> 50.2 us
  local copies, waits for them, and re-layouts: 7.4 us -> 29.1 us
  other arithmetic: 0.01 us -> 20.5 us
    reduce_scatter x7 -> x0, waiting for transfers between devices: 962 us -> none  [the longest x1 313 us: body(): lax.psum_scatter(up_term, 'dp', scatter_dimension=0, tiled=True)]
    ppermute x0 -> x17, waiting for transfers between devices: none -> 51.6 us  [the longest x8 48 us: spread(): came = lax.ppermute(held, 'dp', [(i, i ^ bit) for i in range(n)])]
    all_to_all x0 -> x6, starting transfers between devices: none -> 41.1 us  [the longest x4 30.7 us: exchange(): return lax.all_to_all(values, 'dp', split_axis=0, concat_axis=0, tiled=True)]
    all_to_all x0 -> x6, waiting for transfers between devices: none -> 34.3 us  [the longest x2 18.2 us: spread(): lax.all_to_all(jnp.broadcast_to(both[None], (lines,) + both.shape), 'dp',...]
    all_gather x1 -> x0, waiting for transfers between devices: 13.6 us -> none  [body(): gathered = lax.all_gather(tokens, 'tensor', axis=1, tiled=True)]
    concatenate x0 -> x8, other arithmetic: none -> 11.6 us  [spread(): held = jnp.concatenate([held, came])]
  transfers between devices with their start and end apart: 8 -> 23, of which waited for: 7 -> 8; matrix products, arithmetic and copies ran while one was open for 6% -> 44% of each run, Pallas kernels for 0% -> 0%
where the time goes in v1:
time: 288 us; the launch traced here: 286 us
  matrix products  91.7 us (32%)
  waiting for transfers between devices  85.9 us (30%)
  starting transfers between devices  50.2 us (17%)
  local copies, waits for them, and re-layouts  29.1 us (10%)
  other arithmetic  20.5 us (7%)
  between operations  8.56 us (3%)
    dot_general x12, matrix products, product(): lax.dot_general(left, right, (((left_dim,), (right_dim,)), ((), ())), pre...  91.7 us
    ppermute x8, waiting for transfers between devices, spread(): came = lax.ppermute(held, 'dp', [(i, i ^ bit) for i in range(n)])  48 us
    all_to_all x4, starting transfers between devices, exchange(): return lax.all_to_all(values, 'dp', split_axis=0, concat_axis=0, tiled=True)  30.7 us
    all_to_all x2, waiting for transfers between devices, spread(): lax.all_to_all(jnp.broadcast_to(both[None], (lines,) + both.shape), 'dp',...  18.2 us
    all_to_all x4, waiting for transfers between devices, exchange(): return lax.all_to_all(values, 'dp', split_axis=0, concat_axis=0, tiled=True)  16.1 us
    concatenate x8, other arithmetic, spread(): held = jnp.concatenate([held, came])  11.6 us
    all_to_all x2, starting transfers between devices, spread(): lax.all_to_all(jnp.broadcast_to(both[None], (lines,) + both.shape), 'dp',...  10.4 us
    unnamed x56, local copies, waits for them, and re-layouts  9.3 us
  transfers between devices with their start and end apart: 23, of which 8 were waited for; matrix products, arithmetic and copies ran while one was open for 44% of the time, Pallas kernels for 0%

profile of v1, /device:TPU:10, one launch (start us, length us, event | category | flops | bytes accessed | tf_op | source)
XLA Modules:
  0.0 285.9 jit_solution(12069739267643261071)
XLA Ops:
  2.4 2.6 collective-permute-done
  5.0 5.1 %convolution_convert_fusion = bf16[128,512]{1,0:T(8,128)(2,1)S(1)} fusion(bf16[8192,512]{1,0:T(8,128)(2,1)} %param.11, bf16[128,4096]{0,1:T(8,128)(2,1)S(1)} %collective-permute-done, bf16[128,4096]{0,1:T(8,128)(2,1)S(1)} %copy.50, pred[]{:T(512)S(6)} %eq.5), kind=kOutput, calls=%fused_computation.49 | convolution fusion | flops 1083244544 | bytes 10616833 | tf_op jit(solution)/shard_map/dot_general | solution.py:8
  13.4 5.3 %all-to-all-start.2 = ((bf16[4,2,128,512]{3,2,1,0:T(8,128)(2,1)}), bf16[4,2,128,512]{3,2,1,0:T(8,128)(2,1)S(1)}, u32[]{:S(2)}, u32[]{:S(2)}) async-start(bf16[4,2,128,512]{3,2,1,0:T(8,128)(2,1)} %broadcast_in_dim.5), calls=%async_computation.2 | async-start | bytes 2097152 | tf_op jit(solution)/shard_map/all_to_all | solution.py:47
  18.7 9.0 %fusion.44 = f32[128,7168]{1,0:T(8,128)} fusion(bf16[1024,7168]{1,0:T(8,128)(2,1)} %param.12, bf16[128,512]{1,0:T(8,128)(2,1)S(1)} %collective-permute-done.2, bf16[128,512]{1,0:T(8,128)(2,1)S(1)} %convolution_convert_fusion, pred[]{:T(512)S(6)} %eq.5), kind=kOutput, calls=%fused_computation.90 | convolution fusion | flops 1880227840 | bytes 18612224 | tf_op jit(solution)/shard_map/dot_general | solution.py:8
  27.7 15.0 %fusion.22 = bf16[128,1024]{1,0:T(8,128)(2,1)S(1)} fusion(bf16[1024,7168]{1,0:T(8,128)(2,1)} %param.12, bf16[1024,7168]{1,0:T(8,128)(2,1)} %param.14, bf16[128,7168]{1,0:T(8,128)(2,1)} %param.15, f32[128,7168]{1,0:T(8,128)} %fusion.44, bf16[128,512]{1,0:T(8,128)(2,1)S(1)} %collective-permute-done.1, bf16[128,512]{1,0:T(8,128)(2,1)S(1)} %convolution_convert_fusion.1, ...), kind=kOutput, calls=%fused_computation.47 | convolution fusion | flops 3769499648 | bytes 35389440 | tf_op jit(solution)/shard_map/dot_general | solution.py:8
  42.8 11.8 %fusion.23 = bf16[128,1024]{1,0:T(8,128)(2,1)S(1)} fusion(bf16[1024,7168]{1,0:T(8,128)(2,1)} %param.14, f32[128,7168]{1,0:T(8,128)} %fusion.44, bf16[128,7168]{1,0:T(8,128)(2,1)} %param.15), kind=kOutput, calls=%fused_computation.48 | convolution fusion | flops 1885601792 | bytes 20447232 | tf_op jit(solution)/shard_map/dot_general | solution.py:8
  57.3 5.1 %all-to-all-start.1 = ((bf16[4,2,128,512]{3,2,1,0:T(8,128)(2,1)}), bf16[4,2,128,512]{3,2,1,0:T(8,128)(2,1)S(1)}, u32[]{:S(2)}, u32[]{:S(2)}) async-start(bf16[4,2,128,512]{3,2,1,0:T(8,128)(2,1)} %broadcast_in_dim.4), calls=%async_computation.1 | async-start | bytes 2097152 | tf_op jit(solution)/shard_map/all_to_all | solution.py:47
  62.4 2.4 fusion.28
  64.8 2.3 copy.54
  67.2 18.2 %all-to-all-done.1 = bf16[4,2,128,512]{3,2,1,0:T(8,128)(2,1)S(1)} async-done(((bf16[4,2,128,512]{3,2,1,0:T(8,128)(2,1)}), bf16[4,2,128,512]{3,2,1,0:T(8,128)(2,1)S(1)}, u32[]{:S(2)}, u32[]{:S(2)}) %all-to-all-start.1) | async-done | bytes 1048608 | tf_op jit(solution)/shard_map/all_to_all | solution.py:47
  86.4 7.9 %all-to-all-start = ((bf16[16,128,256]{2,1,0:T(8,128)(2,1)}), bf16[16,128,256]{2,1,0:T(8,128)(2,1)}, u32[]{:S(2)}, u32[]{:S(2)}) async-start(bf16[16,128,256]{2,1,0:T(8,128)(2,1)} %copy.54), calls=%async_computation | async-start | bytes 2097152 | tf_op jit(solution)/shard_map/all_to_all | solution.py:38
  99.9 19.4 %collective-permute-done.12 = bf16[1,4,128,512]{3,2,1,0:T(8,128)(2,1)S(1)} collective-permute-done((bf16[1,4,128,512]{3,2,1,0:T(8,128)(2,1)S(1)}, bf16[1,4,128,512]{3,2,1,0:T(8,128)(2,1)S(1)}, u32[]{:S(2)}, u32[]{:S(2)}) %collective-permute-start.12) | collective-permute-done | bytes 524320 | tf_op jit(solution)/shard_map/ppermute | solution.py:62
  121.7 8.7 %collective-permute-done.7 = bf16[1,4,128,512]{3,2,1,0:T(8,128)(2,1)S(1)} collective-permute-done((bf16[1,4,128,512]{3,2,1,0:T(8,128)(2,1)S(1)}, bf16[1,4,128,512]{3,2,1,0:T(8,128)(2,1)S(1)}, u32[]{:S(2)}, u32[]{:S(2)}) %collective-permute-start.7) | collective-permute-done | bytes 524320 | tf_op jit(solution)/shard_map/ppermute | solution.py:62
  138.5 3.9 %copy.55 = bf16[128,7168]{0,1:T(8,128)(2,1)} copy(bf16[128,7168]{1,0:T(8,128)(2,1)} %param.15) | data formatting | bytes 3670016 | tf_op args[5]
  147.6 8.2 %fusion.72 = f32[128,8192]{1,0:T(8,128)} fusion(bf16[128,512]{1,0:T(8,128)(2,1)S(1)} %add_convert_fusion.1, bf16[8192,512]{1,0:T(8,128)(2,1)} %param.13), kind=kOutput, calls=%fused_computation.120 | convolution fusion | flops 1073741824 | bytes 12713984 | tf_op jit(solution)/shard_map/dot_general | solution.py:8
  157.3 5.5 %all-to-all-start.3 = ((bf16[16,128,448]{1,2,0:T(8,128)(2,1)}), bf16[16,128,448]{1,2,0:T(8,128)(2,1)}, u32[]{:S(2)}, u32[]{:S(2)}) async-start(bf16[16,128,448]{1,2,0:T(8,128)(2,1)} %bitcast.111), calls=%async_computation.3 | async-start | bytes 3670016 | tf_op jit(solution)/shard_map/all_to_all | solution.py:38
  164.4 20.0 %collective-permute-done.8 = bf16[2,4,128,512]{3,2,1,0:T(8,128)(2,1)} collective-permute-done((bf16[2,4,128,512]{3,2,1,0:T(8,128)(2,1)}, bf16[2,4,128,512]{3,2,1,0:T(8,128)(2,1)}, u32[]{:S(2)}, u32[]{:S(2)}) %collective-permute-start.8) | collective-permute-done | bytes 1048608 | tf_op jit(solution)/shard_map/ppermute | solution.py:62
  188.5 2.4 pad_maximum_fusion.6
  196.1 2.8 fusion
  200.5 6.9 %fusion.30 = f32[2048,448]{0,1:T(8,128)} fusion(bf16[1024,7168]{1,0:T(8,128)(2,1)} %param.12, s32[]{:T(128)S(6)} %select_n.208, bf16[2048,512]{1,0:T(8,128)(2,1)} %bitcast.24, bf16[2048,512]{1,0:T(8,128)(2,1)S(1)} %bitcast.117, pred[]{:T(512)S(6)} %eq.5), kind=kOutput, calls=%fused_computation.59 | convolution fusion | flops 1897922560 | bytes 8912901 | tf_op jit(solution)/shard_map/dot_general | solution.py:8
  207.4 7.6 %multiply_convert_fusion = bf16[1024,448]{0,1:T(8,128)(2,1)S(1)} fusion(f32[2048,448]{0,1:T(8,128)} %fusion.30, bf16[2048,512]{1,0:T(8,128)(2,1)} %bitcast.38, bf16[2048,512]{1,0:T(8,128)(2,1)} %bitcast.36, pred[]{:T(512)S(6)} %eq.5, bf16[16,128,448]{1,2,0:T(8,128)(2,1)} %all-to-all-done.3), kind=kOutput, calls=%fused_computation.37 | convolution fusion | flops 1905262592 | bytes 10616833 | tf_op jit(solution)/shard_map/dot_general | solution.py:8
  216.3 11.7 %all-to-all-start.5 = ((bf16[16,64,448]{2,1,0:T(8,128)(2,1)}), bf16[16,64,448]{2,1,0:T(8,128)(2,1)S(1)}, u32[]{:S(2)}, u32[]{:S(2)}) async-start(bf16[16,64,448]{2,1,0:T(8,128)(2,1)} %bitcast.115), calls=%async_computation.5 | async-start | bytes 2097152 | tf_op jit(solution)/shard_map/all_to_all | solution.py:38
  228.0 15.1 %multiply_convert_fusion.1 = bf16[1024,448]{0,1:T(8,128)(2,1)} fusion(f32[2048,448]{0,1:T(8,128)} %fusion.30, bf16[1024,7168]{1,0:T(8,128)(2,1)} %param.14, s32[]{:T(128)S(6)} %select_n.208, bf16[2048,512]{1,0:T(8,128)(2,1)} %bitcast.24, bf16[2048,512]{1,0:T(8,128)(2,1)} %bitcast.118, pred[]{:T(512)S(6)} %eq.5, bf16[2048,512]{1,0:T(8,128)(2,1)} %bitcast.38, ...), kind=kOutput, calls=%fused_computation.38 | convolution fusion | flops 3806855168 | bytes 15861248 | tf_op jit(solution)/shard_map/dot_general | solution.py:8
  243.2 2.3 copy.57
  245.4 7.4 %all-to-all-done.5 = bf16[16,64,448]{2,1,0:T(8,128)(2,1)S(1)} async-done(((bf16[16,64,448]{2,1,0:T(8,128)(2,1)}), bf16[16,64,448]{2,1,0:T(8,128)(2,1)S(1)}, u32[]{:S(2)}, u32[]{:S(2)}) %all-to-all-start.5) | async-done | bytes 917536 | tf_op jit(solution)/shard_map/all_to_all | solution.py:38
  252.8 5.7 %all-to-all-start.4 = ((bf16[16,64,448]{2,1,0:T(8,128)(2,1)}), bf16[16,64,448]{2,1,0:T(8,128)(2,1)}, u32[]{:S(2)}, u32[]{:S(2)}) async-start(bf16[16,64,448]{2,1,0:T(8,128)(2,1)} %bitcast.114), calls=%async_computation.4 | async-start | bytes 2097152 | tf_op jit(solution)/shard_map/all_to_all | solution.py:38
  258.6 2.8 add_convert_fusion
  262.0 4.3 %fusion.21 = bf16[512,512]{1,0:T(8,128)(2,1)} fusion(bf16[2048,512]{1,0:T(8,128)(2,1)S(1)} %bitcast.119, bf16[2048,256]{1,0:T(8,128)(2,1)} %bitcast.6, bf16[2048,256]{1,0:T(8,128)(2,1)} %bitcast.5, pred[]{:T(512)S(6)} %eq.5), kind=kOutput, calls=%fused_computation.46 | convolution fusion | flops 1083703296 | bytes 4718593 | tf_op jit(solution)/shard_map/dot_general | solution.py:8
  266.4 4.3 %fusion.20 = bf16[512,512]{1,0:T(8,128)(2,1)} fusion(bf16[2048,512]{1,0:T(8,128)(2,1)S(1)} %bitcast.120, bf16[2048,256]{1,0:T(8,128)(2,1)} %bitcast.6, bf16[2048,256]{1,0:T(8,128)(2,1)} %bitcast.5, pred[]{:T(512)S(6)} %eq.5), kind=kOutput, calls=%fused_computation.45 | convolution fusion | flops 1083703296 | bytes 4718593 | tf_op jit(solution)/shard_map/dot_general | solution.py:8
  271.3 2.1 reshape.82
  273.4 8.6 %all-to-all-done.4 = bf16[16,64,448]{2,1,0:T(8,128)(2,1)} async-done(((bf16[16,64,448]{2,1,0:T(8,128)(2,1)}), bf16[16,64,448]{2,1,0:T(8,128)(2,1)}, u32[]{:S(2)}, u32[]{:S(2)}) %all-to-all-start.4) | async-done | bytes 917536 | tf_op jit(solution)/shard_map/all_to_all | solution.py:38
  283.8 2.1 reshape.80
  (118 shorter events, 40.8 us)
Async XLA Ops:
  2.3 2.7 collective-permute-start
  10.1 8.6 %collective-permute-start.2 = (bf16[128,512]{1,0:T(8,128)(2,1)S(1)}, bf16[128,512]{1,0:T(8,128)(2,1)S(1)}, u32[]{:S(2)}, u32[]{:S(2)}) collective-permute-start(bf16[128,512]{1,0:T(8,128)(2,1)S(1)} %convolution_convert_fusion), channel_id=1, source_target_pairs={{0,1},{1,0},{2,3},{3,2},{4,5},{5,4},{6,7},{7,6},{8,9},{9,8},{10,11... | collective-permute-start | bytes 393224 | tf_op jit(solution)/shard_map/ppermute | solution.py:16
  11.9 15.8 %collective-permute-start.1 = (bf16[128,512]{1,0:T(8,128)(2,1)S(1)}, bf16[128,512]{1,0:T(8,128)(2,1)S(1)}, u32[]{:S(2)}, u32[]{:S(2)}) collective-permute-start(bf16[128,512]{1,0:T(8,128)(2,1)S(1)} %convolution_convert_fusion.1), channel_id=1, source_target_pairs={{0,1},{1,0},{2,3},{3,2},{4,5},{5,4},{6,7},{7,6},{8,9},{9,8},{10,11... | collective-permute-start | bytes 393224 | tf_op jit(solution)/shard_map/ppermute | solution.py:16
  13.4 42.9 %all-to-all-start.2 = ((bf16[4,2,128,512]{3,2,1,0:T(8,128)(2,1)}), bf16[4,2,128,512]{3,2,1,0:T(8,128)(2,1)S(1)}, u32[]{:S(2)}, u32[]{:S(2)}) async-start(bf16[4,2,128,512]{3,2,1,0:T(8,128)(2,1)} %broadcast_in_dim.5), calls=%async_computation.2 | async-start | bytes 2097152 | tf_op jit(solution)/shard_map/all_to_all | solution.py:47
  42.7 12.4 %collective-permute-start.3 = (bf16[128,512]{1,0:T(8,128)(2,1)S(1)}, bf16[128,512]{1,0:T(8,128)(2,1)S(1)}, u32[]{:S(2)}, u32[]{:S(2)}) collective-permute-start(bf16[128,512]{1,0:T(8,128)(2,1)S(1)} %broadcast_select_fusion.2), channel_id=1, source_target_pairs={{0,1},{1,0},{2,3},{3,2},{4,5},{5,4},{6,7},{7,6},{8,9},{9,8},{10,11... | collective-permute-start | bytes 393224 | tf_op jit(solution)/shard_map/ppermute | solution.py:32
  54.6 1.5 collective-permute-start.4
  57.3 28.1 %all-to-all-start.1 = ((bf16[4,2,128,512]{3,2,1,0:T(8,128)(2,1)}), bf16[4,2,128,512]{3,2,1,0:T(8,128)(2,1)S(1)}, u32[]{:S(2)}, u32[]{:S(2)}) async-start(bf16[4,2,128,512]{3,2,1,0:T(8,128)(2,1)} %broadcast_in_dim.4), calls=%async_computation.1 | async-start | bytes 2097152 | tf_op jit(solution)/shard_map/all_to_all | solution.py:47
  86.4 70.9 %all-to-all-start = ((bf16[16,128,256]{2,1,0:T(8,128)(2,1)}), bf16[16,128,256]{2,1,0:T(8,128)(2,1)}, u32[]{:S(2)}, u32[]{:S(2)}) async-start(bf16[16,128,256]{2,1,0:T(8,128)(2,1)} %copy.54), calls=%async_computation | async-start | bytes 2097152 | tf_op jit(solution)/shard_map/all_to_all | solution.py:38
  94.3 37.2 %copy-start.4 = (bf16[1,4,128,512]{3,2,1,0:T(8,128)(2,1)}, bf16[1,4,128,512]{3,2,1,0:T(8,128)(2,1)S(1)}, u32[]{:S(2)}) copy-start(bf16[1,4,128,512]{3,2,1,0:T(8,128)(2,1)S(1)} %get-tuple-element.23) | copy-start | bytes 1572868
  94.3 24.9 %collective-permute-start.12 = (bf16[1,4,128,512]{3,2,1,0:T(8,128)(2,1)S(1)}, bf16[1,4,128,512]{3,2,1,0:T(8,128)(2,1)S(1)}, u32[]{:S(2)}, u32[]{:S(2)}) collective-permute-start(bf16[1,4,128,512]{3,2,1,0:T(8,128)(2,1)S(1)} %get-tuple-element.23), channel_id=1, source_target_pairs={{0,4},{2,6},{4,0},{6,2},{8,12},{10,14},{12,8},{14,10},{16,20},{18,... | collective-permute-start | bytes 1572872 | tf_op jit(solution)/shard_map/ppermute | solution.py:62
  95.9 24.7 %collective-permute-start.9 = (bf16[1,4,128,512]{3,2,1,0:T(8,128)(2,1)S(1)}, bf16[1,4,128,512]{3,2,1,0:T(8,128)(2,1)S(1)}, u32[]{:S(2)}, u32[]{:S(2)}) collective-permute-start(bf16[1,4,128,512]{3,2,1,0:T(8,128)(2,1)S(1)} %get-tuple-element.24), channel_id=1, source_target_pairs={{0,2},{2,0},{4,6},{6,4},{8,10},{10,8},{12,14},{14,12},{16,18},{18,... | collective-permute-start | bytes 1572872 | tf_op jit(solution)/shard_map/ppermute | solution.py:62
  97.7 32.6 %copy-start.2 = (bf16[1,4,128,512]{3,2,1,0:T(8,128)(2,1)}, bf16[1,4,128,512]{3,2,1,0:T(8,128)(2,1)S(1)}, u32[]{:S(2)}) copy-start(bf16[1,4,128,512]{3,2,1,0:T(8,128)(2,1)S(1)} %get-tuple-element.22) | copy-start | bytes 1572868
  97.7 35.2 %copy-start.24 = (s32[4]{0:T(128)S(1)}, s32[4]{0:T(128)}, u32[]{:S(2)}) copy-start(s32[4]{0:T(128)} %constant.81.clone) | copy-start | bytes 52
  97.8 32.6 %collective-permute-start.7 = (bf16[1,4,128,512]{3,2,1,0:T(8,128)(2,1)S(1)}, bf16[1,4,128,512]{3,2,1,0:T(8,128)(2,1)S(1)}, u32[]{:S(2)}, u32[]{:S(2)}) collective-permute-start(bf16[1,4,128,512]{3,2,1,0:T(8,128)(2,1)S(1)} %get-tuple-element.22), channel_id=1, source_target_pairs={{0,2},{2,0},{4,6},{6,4},{8,10},{10,8},{12,14},{14,12},{16,18},{18,... | collective-permute-start | bytes 1572872 | tf_op jit(solution)/shard_map/ppermute | solution.py:62
  99.3 45.6 %collective-permute-start.15 = (bf16[1,4,128,512]{3,2,1,0:T(8,128)(2,1)S(1)}, bf16[1,4,128,512]{3,2,1,0:T(8,128)(2,1)S(1)}, u32[]{:S(2)}, u32[]{:S(2)}) collective-permute-start(bf16[1,4,128,512]{3,2,1,0:T(8,128)(2,1)S(1)} %get-tuple-element.21), channel_id=1, source_target_pairs={{0,4},{2,6},{4,0},{6,2},{8,12},{10,14},{12,8},{14,10},{16,20},{18,... | collective-permute-start | bytes 1572872 | tf_op jit(solution)/shard_map/ppermute | solution.py:62
  119.2 23.2 %copy-start.21 = (bf16[1,4,128,512]{3,2,1,0:T(8,128)(2,1)}, bf16[1,4,128,512]{3,2,1,0:T(8,128)(2,1)S(1)}, u32[]{:S(2)}) copy-start(bf16[1,4,128,512]{3,2,1,0:T(8,128)(2,1)S(1)} %collective-permute-done.12) | copy-start | bytes 1572868
  120.4 35.4 %collective-permute-start.13 = (bf16[2,4,128,512]{3,2,1,0:T(8,128)(2,1)}, bf16[2,4,128,512]{3,2,1,0:T(8,128)(2,1)}, u32[]{:S(2)}, u32[]{:S(2)}) collective-permute-start(bf16[2,4,128,512]{3,2,1,0:T(8,128)(2,1)} %pad_maximum_fusion.9), channel_id=1, source_target_pairs={{0,2},{2,0},{4,6},{6,4},{8,10},{10,8},{12,14},{14,12},{16,18},{18,... | collective-permute-start | bytes 3145736 | tf_op jit(solution)/shard_map/ppermute | solution.py:62
  120.5 21.9 %copy-start.18 = (bf16[1,4,128,512]{3,2,1,0:T(8,128)(2,1)}, bf16[1,4,128,512]{3,2,1,0:T(8,128)(2,1)S(1)}, u32[]{:S(2)}) copy-start(bf16[1,4,128,512]{3,2,1,0:T(8,128)(2,1)S(1)} %collective-permute-done.9) | copy-start | bytes 1572868
  121.7 41.1 %collective-permute-start.10 = (bf16[2,4,128,512]{3,2,1,0:T(8,128)(2,1)}, bf16[2,4,128,512]{3,2,1,0:T(8,128)(2,1)}, u32[]{:S(2)}, u32[]{:S(2)}) collective-permute-start(bf16[2,4,128,512]{3,2,1,0:T(8,128)(2,1)} %pad_maximum_fusion.10), channel_id=1, source_target_pairs={{0,4},{2,6},{4,0},{6,2},{8,12},{10,14},{12,8},{14,10},{16,20},{18,... | collective-permute-start | bytes 3145736 | tf_op jit(solution)/shard_map/ppermute | solution.py:62
  130.3 15.8 %copy-start.19 = (bf16[1,4,128,512]{3,2,1,0:T(8,128)(2,1)}, bf16[1,4,128,512]{3,2,1,0:T(8,128)(2,1)S(1)}, u32[]{:S(2)}) copy-start(bf16[1,4,128,512]{3,2,1,0:T(8,128)(2,1)S(1)} %collective-permute-done.7) | copy-start | bytes 1572868
  131.5 52.9 %collective-permute-start.8 = (bf16[2,4,128,512]{3,2,1,0:T(8,128)(2,1)}, bf16[2,4,128,512]{3,2,1,0:T(8,128)(2,1)}, u32[]{:S(2)}, u32[]{:S(2)}) collective-permute-start(bf16[2,4,128,512]{3,2,1,0:T(8,128)(2,1)} %pad_maximum_fusion.8), channel_id=1, source_target_pairs={{0,4},{2,6},{4,0},{6,2},{8,12},{10,14},{12,8},{14,10},{16,20},{18,... | collective-permute-start | bytes 3145736 | tf_op jit(solution)/shard_map/ppermute | solution.py:62
  146.1 41.7 %collective-permute-start.16 = (bf16[2,4,128,512]{3,2,1,0:T(8,128)(2,1)}, bf16[2,4,128,512]{3,2,1,0:T(8,128)(2,1)}, u32[]{:S(2)}, u32[]{:S(2)}) collective-permute-start(bf16[2,4,128,512]{3,2,1,0:T(8,128)(2,1)} %pad_maximum_fusion.11), channel_id=1, source_target_pairs={{0,2},{2,0},{4,6},{6,4},{8,10},{10,8},{12,14},{14,12},{16,18},{18,... | collective-permute-start | bytes 3145736 | tf_op jit(solution)/shard_map/ppermute | solution.py:62
  157.3 50.2 %all-to-all-start.3 = ((bf16[16,128,448]{1,2,0:T(8,128)(2,1)}), bf16[16,128,448]{1,2,0:T(8,128)(2,1)}, u32[]{:S(2)}, u32[]{:S(2)}) async-start(bf16[16,128,448]{1,2,0:T(8,128)(2,1)} %bitcast.111), calls=%async_computation.3 | async-start | bytes 3670016 | tf_op jit(solution)/shard_map/all_to_all | solution.py:38
  162.8 21.6 %copy-start.3 = (bf16[1,4,128,512]{3,2,1,0:T(8,128)(2,1)S(1)}, bf16[1,4,128,512]{3,2,1,0:T(8,128)(2,1)}, u32[]{:S(2)}) copy-start(bf16[1,4,128,512]{3,2,1,0:T(8,128)(2,1)} %copy-done.2) | copy-start | bytes 1572868
  162.8 21.6 %copy-start.20 = (bf16[1,4,128,512]{3,2,1,0:T(8,128)(2,1)S(1)}, bf16[1,4,128,512]{3,2,1,0:T(8,128)(2,1)}, u32[]{:S(2)}) copy-start(bf16[1,4,128,512]{3,2,1,0:T(8,128)(2,1)} %copy-done.19) | copy-start | bytes 1572868
  187.7 12.8 %copy-start.7 = (bf16[4,4,128,512]{3,2,1,0:T(8,128)(2,1)}, bf16[4,4,128,512]{3,2,1,0:T(8,128)(2,1)S(1)}, u32[]{:S(2)}) copy-start(bf16[4,4,128,512]{3,2,1,0:T(8,128)(2,1)S(1)} %pad_maximum_fusion.5) | copy-start | bytes 6291460
  187.7 12.8 %collective-permute-start.11 = (bf16[16,128,512]{2,1,0:T(8,128)(2,1)S(1)}, bf16[16,128,512]{2,1,0:T(8,128)(2,1)}, u32[]{:S(2)}, u32[]{:S(2)}) collective-permute-start(bf16[16,128,512]{2,1,0:T(8,128)(2,1)S(1)} %bitcast.116), channel_id=1, source_target_pairs={{0,1},{1,0},{2,3},{3,2},{4,5},{5,4},{6,7},{7,6},{8,9},{9,8},{10,11... | collective-permute-start | bytes 6291464 | tf_op jit(solution)/shard_map/ppermute | solution.py:16
  194.0 13.4 %collective-permute-start.14 = (bf16[16,128,512]{2,1,0:T(8,128)(2,1)}, bf16[16,128,512]{2,1,0:T(8,128)(2,1)}, u32[]{:S(2)}, u32[]{:S(2)}) collective-permute-start(bf16[16,128,512]{2,1,0:T(8,128)(2,1)} %bitcast.37), channel_id=1, source_target_pairs={{0,1},{1,0},{2,3},{3,2},{4,5},{5,4},{6,7},{7,6},{8,9},{9,8},{10,11... | collective-permute-start | bytes 6291464 | tf_op jit(solution)/shard_map/ppermute | solution.py:16
  200.0 58.6 %collective-permute-start.5 = (bf16[128,4096]{1,0:T(8,128)(2,1)}, bf16[128,4096]{1,0:T(8,128)(2,1)}, u32[]{:S(2)}, u32[]{:S(2)}) collective-permute-start(bf16[128,4096]{1,0:T(8,128)(2,1)} %broadcast_select_fusion), channel_id=1, source_target_pairs={{0,1},{1,0},{2,3},{3,2},{4,5},{5,4},{6,7},{7,6},{8,9},{9,8},{10,11... | collective-permute-start | bytes 3145736 | tf_op jit(solution)/shard_map/ppermute | solution.py:32
  200.0 62.0 %collective-permute-start.6 = (bf16[16,128,256]{2,1,0:T(8,128)(2,1)}, bf16[16,128,256]{2,1,0:T(8,128)(2,1)}, u32[]{:S(2)}, u32[]{:S(2)}) collective-permute-start(bf16[16,128,256]{2,1,0:T(8,128)(2,1)} %all-to-all-done), channel_id=1, source_target_pairs={{0,1},{1,0},{2,3},{3,2},{4,5},{5,4},{6,7},{7,6},{8,9},{9,8},{10,11... | collective-permute-start | bytes 3145736 | tf_op jit(solution)/shard_map/ppermute | solution.py:16
  216.3 36.5 %all-to-all-start.5 = ((bf16[16,64,448]{2,1,0:T(8,128)(2,1)}), bf16[16,64,448]{2,1,0:T(8,128)(2,1)S(1)}, u32[]{:S(2)}, u32[]{:S(2)}) async-start(bf16[16,64,448]{2,1,0:T(8,128)(2,1)} %bitcast.115), calls=%async_computation.5 | async-start | bytes 2097152 | tf_op jit(solution)/shard_map/all_to_all | solution.py:38
  252.8 29.1 %all-to-all-start.4 = ((bf16[16,64,448]{2,1,0:T(8,128)(2,1)}), bf16[16,64,448]{2,1,0:T(8,128)(2,1)}, u32[]{:S(2)}, u32[]{:S(2)}) async-start(bf16[16,64,448]{2,1,0:T(8,128)(2,1)} %bitcast.114), calls=%async_computation.4 | async-start | bytes 2097152 | tf_op jit(solution)/shard_map/all_to_all | solution.py:38
  (18 other events, 83.9 us)

commit v2 on v1

--- a/solution.py
+++ b/solution.py
@@ -1,7 +1,13 @@
+import functools
+
 import jax
 import jax.numpy as jnp
 from jax import lax
+from jax.experimental import pallas as pl
+from jax.experimental.pallas import tpu as pltpu
 from jax.sharding import PartitionSpec as P
+
+LINES = 4
 
 
 def product(left, right, left_dim, right_dim):
@@ -40,7 +46,7 @@
 
 def spread(first, second):
     n = lax.axis_size("dp")
-    lines = 4
+    lines = LINES
     plane = n // lines
     both = jnp.stack([first, second])
     groups = [[a * plane + b for a in range(lines)] for b in range(plane)]
@@ -80,7 +86,7 @@
     return gate_delta, up_delta
 
 
-def body(tokens, gate_left, gate_right, up_left, up_right, hidden_grad):
+def general(tokens, gate_left, gate_right, up_left, up_right, hidden_grad):
     n, cores = lax.axis_size("dp"), lax.axis_size("tensor")
     here, core = lax.axis_index("dp"), lax.axis_index("tensor")
     rows, units = hidden_grad.shape
@@ -139,6 +145,424 @@
     )
 
 
+def pair(values):
+    return lax.ppermute(values, "tensor", [(0, 1), (1, 0)])
+
+
+def local_kernel(core_ref, own_ref, other_ref, gate_w_ref, up_w_ref, hidden_ref, keep_ref, send_ref, codes, sums):
+    step = pl.program_id(0)
+    core = core_ref[0]
+    half = own_ref.shape[2]
+
+    @pl.when(step == 0)
+    def _():
+        sums[...] = jnp.zeros_like(sums)
+        codes[core] = own_ref[...]
+        codes[1 - core] = other_ref[...]
+
+    gate_w, up_w = gate_w_ref[...], up_w_ref[...]
+    gate_pre = jnp.dot(codes[0, 0], gate_w[:half], preferred_element_type=jnp.float32)
+    gate_pre += jnp.dot(codes[1, 0], gate_w[half:], preferred_element_type=jnp.float32)
+    up_pre = jnp.dot(codes[0, 1], up_w[:half], preferred_element_type=jnp.float32)
+    up_pre += jnp.dot(codes[1, 1], up_w[half:], preferred_element_type=jnp.float32)
+    gate_delta, up_delta = deltas(gate_pre, up_pre, hidden_ref[...].astype(jnp.float32))
+    for which, delta, weight in ((0, gate_delta, gate_w), (1, up_delta, up_w)):
+        for side in range(2):
+            sums[side, which] += product(delta, weight[side * half : (side + 1) * half], 1, 1)
+
+    @pl.when(step == pl.num_programs(0) - 1)
+    def _():
+        keep_ref[...] = sums[core]
+        send_ref[...] = sums[1 - core].astype(send_ref.dtype)
+
+
+def local_ranks(core, own, other, gate_right, up_right, hidden_grad, block):
+    rank, units = gate_right.shape
+    rows = hidden_grad.shape[0]
+    whole = pl.BlockSpec(own.shape, lambda i, c: (0, 0, 0))
+    weight = pl.BlockSpec((rank, block), lambda i, c: (0, i))
+    return pl.pallas_call(
+        local_kernel,
+        name="local_ranks",
+        out_shape=(
+            jax.ShapeDtypeStruct(own.shape, jnp.float32),
+            jax.ShapeDtypeStruct(own.shape, jnp.bfloat16),
+        ),
+        grid_spec=pltpu.PrefetchScalarGridSpec(
+            num_scalar_prefetch=1,
+            grid=(units // block,),
+            in_specs=[whole, whole, weight, weight, pl.BlockSpec((rows, block), lambda i, c: (0, i))],
+            out_specs=[whole, whole],
+            scratch_shapes=[
+                pltpu.VMEM((2,) + own.shape, jnp.bfloat16),
+                pltpu.VMEM((2,) + own.shape, jnp.float32),
+            ],
+        ),
+        compiler_params=pltpu.CompilerParams(dimension_semantics=("arbitrary",)),
+        cost_estimate=pl.CostEstimate(
+            flops=8 * rows * rank * units,
+            transcendentals=2 * rows * units,
+            bytes_accessed=4 * rank * units + 2 * rows * units,
+        ),
+    )(core[None], own, other, gate_right, up_right, hidden_grad)
+
+
+def weights_kernel(where_ref, gate_ref, up_ref, out_ref, window, sems):
+    core, shift = where_ref[0], where_ref[2]
+    width = window.shape[2]
+    half, share = out_ref.shape[2] // 2, out_ref.shape[1]
+    start = pl.multiple_of(where_ref[1], 128)
+    copies = [
+        pltpu.make_async_copy(ref.at[:, pl.ds(start, width)], window.at[i], sems.at[i])
+        for i, ref in enumerate((gate_ref, up_ref))
+    ]
+    for copy in copies:
+        copy.start()
+    for i, copy in enumerate(copies):
+        copy.wait()
+        for side in range(2):
+            first = pl.multiple_of((core if side == 0 else 1 - core) * half, half)
+            turned = window[i, pl.ds(first, half), :].T
+            low, high = turned[:share], turned[width - share :]
+            out_ref[i, :, side * half : (side + 1) * half] = jnp.where(shift == 0, low, high)
+
+
+def weight_slices(core, here, gate_right, up_right, share):
+    rank = gate_right.shape[0]
+    width = -(-share // 128) * 128
+    start = here * share
+    where = jnp.stack([core, start // 128 * 128, start % 128]).astype(jnp.int32)
+    return pl.pallas_call(
+        weights_kernel,
+        name="weight_slices",
+        out_shape=jax.ShapeDtypeStruct((2, share, rank), jnp.bfloat16),
+        in_specs=[
+            pl.BlockSpec(memory_space=pltpu.SMEM),
+            pl.BlockSpec(memory_space=pl.ANY),
+            pl.BlockSpec(memory_space=pl.ANY),
+        ],
+        out_specs=pl.BlockSpec(memory_space=pltpu.VMEM),
+        scratch_shapes=[
+            pltpu.VMEM((2, rank, width), jnp.bfloat16),
+            pltpu.SemaphoreType.DMA((2,)),
+        ],
+        cost_estimate=pl.CostEstimate(
+            flops=0, transcendentals=0, bytes_accessed=8 * rank * share
+        ),
+    )(where, gate_right, up_right)
+
+
+def pack_kernel(core_ref, own_ref, other_ref, out_ref):
+    core = core_ref[0]
+    blocks, width = out_ref.shape[:2]
+    from_own = (pl.program_id(0) >= pl.num_programs(0) // 2) == (core == 1)
+
+    def move(source):
+        for i in range(blocks):
+            first = pl.multiple_of((2 * i + core) * width, width)
+            out_ref[i] = source[:, pl.ds(first, width)].T
+
+    pl.when(from_own)(lambda: move(own_ref))
+    pl.when(jnp.logical_not(from_own))(lambda: move(other_ref))
+
+
+def pack_tokens(core, own, other, n):
+    rows, local = own.shape
+    width = local // n
+    steps = 4
+    block = pl.BlockSpec((rows, 2 * local // steps), lambda i, c: (0, i % (steps // 2)))
+    return pl.pallas_call(
+        pack_kernel,
+        name="pack_tokens",
+        out_shape=jax.ShapeDtypeStruct((n, width, rows), own.dtype),
+        grid_spec=pltpu.PrefetchScalarGridSpec(
+            num_scalar_prefetch=1,
+            grid=(steps,),
+            in_specs=[block, block],
+            out_specs=pl.BlockSpec((n // steps, width, rows), lambda i, c: (i, 0, 0)),
+        ),
+        cost_estimate=pl.CostEstimate(
+            flops=0, transcendentals=0, bytes_accessed=6 * rows * local
+        ),
+    )(core[None], own, other)
+
+
+def right_kernel(scale, first, last, where_ref, *refs):
+    if last:
+        sides = ((refs[0], refs[2]), (refs[1], refs[3]))
+        read = lambda ref, i: ref[...]
+        rest = refs[4:]
+    else:
+        sides = (refs[:2], refs[:2])
+        read = lambda ref, i: ref[i]
+        rest = refs[2:]
+    hidden, weights = rest[:2]
+    held = None if first else rest[2]
+    out = refs[-1]
+    share, half = weights.shape[1], weights.shape[2] // 2
+    lines = hidden.shape[0]
+    codes = [
+        jnp.concatenate([read(ref, i).reshape(-1, half) for ref in sides[i]], 1) for i in range(2)
+    ]
+    gate_pre, up_pre = [product(weights[i], codes[i], 1, 1) for i in range(2)]
+    block = where_ref[1]
+    upstream = jnp.concatenate(
+        [hidden[(where_ref[2] + lines - i) % lines, block] for i in range(lines)], 1
+    ).astype(jnp.float32)
+    both = deltas(gate_pre, up_pre, upstream)
+    for side in range(2):
+        parts = []
+        for i in range(2):
+            term = product(both[i], codes[i][:, side * half : (side + 1) * half], 1, 0)
+            if not first:
+                term += held[side, i * share : (i + 1) * share]
+            if last:
+                parts.append(term * scale)
+            else:
+                out[side, i * share : (i + 1) * share] = term
+        if last:
+            done = jnp.concatenate(parts, 0).T.astype(out.dtype)
+            place = where_ref[0] if side == 0 else 1 - where_ref[0]
+            blocks = out.shape[0] // 2
+            out[pl.ds(place * blocks, blocks)] = done.reshape((blocks,) + out.shape[1:])
+
+
+def right_part(where, pieces, sums, last, hidden, weights, scale, n):
+    share, half = weights.shape[1], weights.shape[2] // 2
+    lines, rows = hidden.shape[0], hidden.shape[3]
+    vmem = pl.BlockSpec(memory_space=pltpu.VMEM)
+    operands = list(pieces) + [hidden, weights] + ([] if sums is None else [sums])
+    if last:
+        out_shape = jax.ShapeDtypeStruct((n, 2 * half // n, 2 * share), jnp.bfloat16)
+    else:
+        out_shape = jax.ShapeDtypeStruct((2, 2 * share, half), jnp.float32)
+    return pl.pallas_call(
+        functools.partial(right_kernel, scale, sums is None, last),
+        name="right_last" if last else "right_part",
+        out_shape=out_shape,
+        in_specs=[pl.BlockSpec(memory_space=pltpu.SMEM)] + [vmem] * len(operands),
+        out_specs=vmem,
+        input_output_aliases={} if sums is None or last else {5: 0},
+        cost_estimate=pl.CostEstimate(
+            flops=16 * lines * rows * half * share,
+            transcendentals=2 * lines * rows * share,
+            bytes_accessed=8 * lines * rows * half + 8 * share * half,
+        ),
+    )(where, *operands)
+
+
+def settle_kernel(in_ref, gate_ref, up_ref):
+    width = in_ref.shape[2]
+    first = lax.broadcasted_iota(jnp.int32, in_ref.shape[1:], 1) < width // 2
+    for i in range(in_ref.shape[0] // 2):
+        even, odd = in_ref[2 * i].astype(jnp.float32), in_ref[2 * i + 1].astype(jnp.float32)
+        columns = slice(i * width, (i + 1) * width)
+        gate = jnp.where(first, even, pltpu.roll(odd, width // 2, 1))
+        up = jnp.where(first, pltpu.roll(even, width // 2, 1), odd)
+        gate_ref[:, columns] = gate.astype(gate_ref.dtype)
+        up_ref[:, columns] = up.astype(up_ref.dtype)
+
+
+def settle(blocks):
+    n, rows, width = blocks.shape
+    vmem = pl.BlockSpec(memory_space=pltpu.VMEM)
+    shape = jax.ShapeDtypeStruct((rows, n * width // 2), blocks.dtype)
+    return pl.pallas_call(
+        settle_kernel,
+        name="settle",
+        out_shape=(shape, shape),
+        in_specs=[vmem],
+        out_specs=(vmem, vmem),
+        cost_estimate=pl.CostEstimate(
+            flops=0, transcendentals=0, bytes_accessed=4 * n * rows * width
+        ),
+    )(blocks)
+
+
+def input_kernel(core_ref, ranks_ref, gate_ref, up_ref, send_ref, keep_ref):
+    step = pl.program_id(0)
+    half = pl.num_programs(0) // 2
+    terms = product(ranks_ref[0], gate_ref[...], 1, 1) + product(ranks_ref[1], up_ref[...], 1, 1)
+
+    @pl.when(step < half)
+    def _():
+        send_ref[...] = terms.astype(send_ref.dtype)
+
+    @pl.when(step >= half)
+    def _():
+        keep_ref[...] = terms
+
+
+def input_terms(core, ranks, gate_left, up_left):
+    features, half = gate_left.shape
+    rows = ranks.shape[1]
+    steps = 8
+    block = features // steps
+    weight = pl.BlockSpec((block, half), lambda i, c: ((i + (1 - c[0]) * (steps // 2)) % steps, 0))
+    return pl.pallas_call(
+        input_kernel,
+        name="input_terms",
+        out_shape=(
+            jax.ShapeDtypeStruct((rows, features // 2), jnp.bfloat16),
+            jax.ShapeDtypeStruct((rows, features // 2), jnp.float32),
+        ),
+        grid_spec=pltpu.PrefetchScalarGridSpec(
+            num_scalar_prefetch=1,
+            grid=(steps,),
+            in_specs=[pl.BlockSpec(ranks.shape, lambda i, c: (0, 0, 0)), weight, weight],
+            out_specs=[
+                pl.BlockSpec((rows, block), lambda i, c: (0, jnp.minimum(i, steps // 2 - 1))),
+                pl.BlockSpec((rows, block), lambda i, c: (0, jnp.maximum(i - steps // 2, 0))),
+            ],
+        ),
+        compiler_params=pltpu.CompilerParams(dimension_semantics=("arbitrary",)),
+        cost_estimate=pl.CostEstimate(
+            flops=4 * rows * half * features,
+            transcendentals=0,
+            bytes_accessed=4 * half * features + 6 * rows * features // 2,
+        ),
+    )(core[None], ranks, gate_left, up_left)
+
+
+def left_kernel(scale, where_ref, own, other, *refs):
+    pieces, (gate_out, up_out) = refs[:-2], refs[-2:]
+    core = where_ref[0]
+    lines, half = pieces[0].shape[1], pieces[0].shape[3]
+    width = own.shape[2]
+    ranks = [[piece[i] for piece in pieces[:3]] + [pieces[3 + i][...]] for i in range(2)]
+    for side, source in ((0, own), (1, other)):
+        sums = [0.0, 0.0]
+        for offset in range(4):
+            block = where_ref[1] ^ offset
+            values = jnp.concatenate(
+                [source[(where_ref[2] + lines - i) % lines, block] for i in range(lines)], 1
+            )
+            for i in range(2):
+                sums[i] += product(values, ranks[i][offset].reshape(-1, half), 1, 0)
+        start = pl.multiple_of((core if side == 0 else 1 - core) * width, width)
+        for out, result in ((gate_out, sums[0]), (up_out, sums[1])):
+            out[pl.ds(start, width), :] = (result * scale).astype(out.dtype)
+
+
+def left_grads(where, own, other, pieces, scale):
+    width, half = own.shape[2], pieces[0].shape[3]
+    vmem = pl.BlockSpec(memory_space=pltpu.VMEM)
+    shape = jax.ShapeDtypeStruct((2 * width, half), jnp.bfloat16)
+    tokens = own.shape[0] * own.shape[1] * own.shape[3]
+    return pl.pallas_call(
+        functools.partial(left_kernel, scale),
+        name="left_grads",
+        out_shape=(shape, shape),
+        in_specs=[pl.BlockSpec(memory_space=pltpu.SMEM)] + [vmem] * (2 + len(pieces)),
+        out_specs=(vmem, vmem),
+        cost_estimate=pl.CostEstimate(
+            flops=8 * width * half * tokens,
+            transcendentals=0,
+            bytes_accessed=4 * width * tokens + 4 * half * tokens,
+        ),
+    )(where, own, other, *pieces)
+
+
+def line_gather(values):
+    n = lax.axis_size("dp")
+    plane = n // LINES
+    return [values] + [
+        lax.ppermute(values, "dp", [(i, (i + shift * plane) % n) for i in range(n)])
+        for shift in range(1, LINES)
+    ]
+
+
+def stacked(line):
+    return jnp.stack([jnp.stack([values[i] for values in line]) for i in range(2)])
+
+
+def hop(values, bit):
+    return lax.ppermute(values, "dp", [(i, i ^ bit) for i in range(lax.axis_size("dp"))])
+
+
+def after(value, *others):
+    return lax.optimization_barrier((value, *others))[0]
+
+
+def fast(tokens, gate_left, gate_right, up_left, up_right, hidden_grad):
+    n = lax.axis_size("dp")
+    here, core = lax.axis_index("dp"), lax.axis_index("tensor")
+    rows, units = hidden_grad.shape
+    share, plane = units // n, n // LINES
+    scale = float(rows * n) ** (-0.5)
+    where = [
+        jnp.stack([core, (here % plane) ^ offset, here // plane]).astype(jnp.int32)
+        for offset in range(plane)
+    ]
+
+    hidden_all = exchange(hidden_grad.T.reshape(n, share, rows)).reshape(LINES, plane, share, rows)
+
+    other = pair(tokens)
+    gathered = jnp.where(
+        core == 0,
+        jnp.concatenate([tokens, other], 1),
+        jnp.concatenate([other, tokens], 1),
+    )
+    parts = jnp.stack(
+        [
+            product(gathered, gate_left, 1, 0).astype(jnp.bfloat16),
+            product(gathered, up_left, 1, 0).astype(jnp.bfloat16),
+        ]
+    )
+    line = line_gather(parts)
+    packed = pack_tokens(core, tokens, other, n)
+    weights = weight_slices(core, here, gate_right, up_right, share)
+
+    parts_other = pair(parts)
+    keep, send = local_ranks(
+        core, after(parts, packed, weights), parts_other, gate_right, up_right, hidden_grad, 512
+    )
+    own = stacked(after(line, keep))
+    ranks = (keep + pair(send).astype(jnp.float32)).astype(jnp.bfloat16)
+
+    codes_x, codes_y, own_pair = hop(own, 1), hop(own, 2), pair(own)
+    rank_line = line_gather(after(ranks, own_pair))
+    send, keep = input_terms(core, after(ranks, own_pair), gate_left, up_left)
+    input_pair = pair(send)
+    mine = exchange(after(packed, keep))
+
+    part = functools.partial(right_part, hidden=hidden_all, weights=weights, scale=scale, n=n)
+    sums = part(where[0], (after(own, keep), own_pair), sums=None, last=False)
+    codes_x, codes_y, rank_line, sums = lax.optimization_barrier(
+        (codes_x, codes_y, rank_line, sums)
+    )
+    gate_xy, up_xy = hop(codes_x[0], 2), hop(codes_y[1], 1)
+    x_pair, y_pair = pair(codes_x), pair(codes_y)
+    rank_own = stacked(rank_line)
+    rank_x, rank_y = hop(rank_own, 1), hop(rank_own, 2)
+    sums = part(where[1], (codes_x, x_pair), sums=sums, last=False)
+    sums = part(where[2], (codes_y, y_pair), sums=sums, last=False)
+    gate_xy, up_xy, sums = lax.optimization_barrier((gate_xy, up_xy, sums))
+    pieces = (gate_xy, up_xy, pair(gate_xy), pair(up_xy))
+    sums = part(where[3], pieces, sums=sums, last=True)
+    rank_x, rank_y, sums = lax.optimization_barrier((rank_x, rank_y, sums))
+    gate_xy, up_xy = hop(rank_x[0], 2), hop(rank_y[1], 1)
+    finished = exchange(sums)
+
+    input_grad = (keep + input_pair.astype(jnp.float32)).astype(jnp.bfloat16)
+    mine = mine.reshape((LINES, plane) + packed.shape[1:])
+    gate_left_grad, up_left_grad = left_grads(
+        where[0], mine, pair(mine), (rank_own, rank_x, rank_y, gate_xy, up_xy), scale
+    )
+    gate_grad, up_grad = settle(finished)
+    return input_grad, gate_left_grad, gate_grad, up_left_grad, up_grad
+
+
+def body(tokens, gate_left, gate_right, up_left, up_right, hidden_grad):
+    n, cores = lax.axis_size("dp"), lax.axis_size("tensor")
+    fits = n == 4 * LINES and cores == 2 and tokens.shape[0] % 128 == 0
+    fits = fits and hidden_grad.shape[1] % (n * 16) == 0 and hidden_grad.shape[1] % 512 == 0
+    fits = fits and gate_left.shape[1] % 128 == 0 and gate_left.shape[0] % (n * 256) == 0
+    fits = fits and hidden_grad.shape[1] // n % 128 in (0, 64)
+    chosen = fast if fits else general
+    return chosen(tokens, gate_left, gate_right, up_left, up_right, hidden_grad)
+
+
 def solution(mesh):
     placed = (
         P("dp", "tensor"),

time: 288 us -> 214 us (0.74)
  Pallas kernels: 0 us -> 81.6 us
  matrix products: 91.7 us -> 10.7 us
  waiting for transfers between devices: 85.9 us -> 54.7 us
  other arithmetic: 20.5 us -> 7.53 us
  starting transfers between devices: 50.2 us -> 37.5 us
  local copies, waits for them, and re-layouts: 29.1 us -> 18.5 us
  between operations: 8.56 us -> 0.92 us
    pallas_call x0 -> x10, Pallas kernels: none -> 81.6 us  [the longest x4 30 us: right_part(): pl.pallas_call(functools.partial(right_kernel, scale, sums is None, last)...]
    dot_general x12 -> x2, matrix products: 91.7 us -> 10.7 us  [product(): lax.dot_general(left, right, (((left_dim,), (right_dim,)), ((), ())), pre...]
    all_to_all x2 -> x0, waiting for transfers between devices: 18.2 us -> none  [spread(): lax.all_to_all(jnp.broadcast_to(both[None], (lines,) + both.shape), 'dp',...]
    all_to_all x4 -> x3, starting transfers between devices: 30.7 us -> 18.1 us  [exchange(): return lax.all_to_all(values, 'dp', split_axis=0, concat_axis=0, tiled=True)]
    concatenate x8 -> x0, other arithmetic: 11.6 us -> none  [spread(): held = jnp.concatenate([held, came])]
    all_to_all x2 -> x0, starting transfers between devices: 10.4 us -> none  [spread(): lax.all_to_all(jnp.broadcast_to(both[None], (lines,) + both.shape), 'dp',...]
    ppermute x17 -> x24, starting transfers between devices: 9.12 us -> 19.4 us  [the longest x8 9.35 us: hop(): lax.ppermute(values, 'dp', [(i, i ^ bit) for i in range(lax.axis_size('dp...]
    all_to_all x4 -> x3, waiting for transfers between devices: 16.1 us -> 8 us  [exchange(): return lax.all_to_all(values, 'dp', split_axis=0, concat_axis=0, tiled=True)]
  transfers between devices with their start and end apart: 23 -> 27, of which waited for: 8 -> 9; matrix products, arithmetic and copies ran while one was open for 44% -> 15% of each run, Pallas kernels for 0% -> 37%
where the time goes in v2:
time: 214 us; the launch traced here: 211 us
  Pallas kernels  81.6 us (38%)
  waiting for transfers between devices  54.7 us (26%)
  starting transfers between devices  37.5 us (18%)
  local copies, waits for them, and re-layouts  18.5 us (9%)
  matrix products  10.7 us (5%)
  other arithmetic  7.53 us (4%)
    pallas_call x4, Pallas kernels, right_part(): pl.pallas_call(functools.partial(right_kernel, scale, sums is None, last)...  30 us
    ppermute x8, waiting for transfers between devices, hop(): lax.ppermute(values, 'dp', [(i, i ^ bit) for i in range(lax.axis_size('dp...  24.7 us
    pallas_call x1, Pallas kernels, local_ranks(): pl.pallas_call(local_kernel, name='local_ranks', out_shape=(jax.ShapeDtyp...  22.4 us
    ppermute x6, waiting for transfers between devices, line_gather(): lax.ppermute(values, 'dp', [(i, (i + shift * plane) % n) for i in range(n)])  20.5 us
    all_to_all x3, starting transfers between devices, exchange(): return lax.all_to_all(values, 'dp', split_axis=0, concat_axis=0, tiled=True)  18.1 us
    pallas_call x1, Pallas kernels, input_terms(): pl.pallas_call(input_kernel, name='input_terms', out_shape=(jax.ShapeDtyp...  12.1 us
    dot_general x2, matrix products, product(): lax.dot_general(left, right, (((left_dim,), (right_dim,)), ((), ())), pre...  10.7 us
    ppermute x8, starting transfers between devices, hop(): lax.ppermute(values, 'dp', [(i, i ^ bit) for i in range(lax.axis_size('dp...  9.35 us
  transfers between devices with their start and end apart: 27, of which 9 were waited for; matrix products, arithmetic and copies ran while one was open for 15% of the time, Pallas kernels for 37%

profile of v2, /device:TPU:10, one launch (start us, length us, event | category | flops | bytes accessed | tf_op | source)
XLA Modules:
  0.0 211.5 jit_solution(12107332109415032827)
XLA Ops:
  0.7 4.0 %copy.14 = bf16[128,7168]{0,1:T(8,128)(2,1)} copy(bf16[128,7168]{1,0:T(8,128)(2,1)} %hidden_ref.1) | data formatting | bytes 3670016 | tf_op args[5]
  4.7 7.3 %all-to-all-start.1 = ((bf16[16,448,128]{2,1,0:T(8,128)(2,1)}), bf16[16,448,128]{2,1,0:T(8,128)(2,1)S(1)}, u32[]{:S(2)}, u32[]{:S(2)}) async-start(bf16[16,448,128]{2,1,0:T(8,128)(2,1)} %bitcast.39), calls=%async_computation.1 | async-start | bytes 3670016 | tf_op jit(solution)/shard_map/all_to_all | solution.py:44
  12.0 5.3 %fusion = bf16[1,128,512]{2,1,0:T(8,128)(2,1)S(1)} fusion(bf16[8192,512]{1,0:T(8,128)(2,1)} %gate_ref.3, bf16[128,4096]{1,0:T(8,128)(2,1)} %collective-permute-done.other_ref, bf16[128,4096]{1,0:T(8,128)(2,1)S(1)} %copy-done.7, pred[]{:T(512)S(6)} %eq.9), kind=kOutput, calls=%fused_computation.4 | convolution fusion | flops 1083244544 | bytes 10616833 | tf_op jit(solution)/shard_map/dot_general | solution.py:14
  17.3 5.5 %fusion.1 = bf16[1,128,512]{2,1,0:T(8,128)(2,1)S(1)} fusion(bf16[8192,512]{1,0:T(8,128)(2,1)} %up_ref.3, bf16[128,4096]{1,0:T(8,128)(2,1)} %collective-permute-done.other_ref, bf16[128,4096]{1,0:T(8,128)(2,1)S(1)} %copy-done.7, pred[]{:T(512)S(6)} %eq.9), kind=kOutput, calls=%fused_computation.5 | convolution fusion | flops 1083244544 | bytes 10616833 | tf_op jit(solution)/shard_map/dot_general | solution.py:14
  24.1 3.8 %weight_slices.1.refs_3_.refs_5_ = bf16[2,448,1024]{2,1,0:T(8,128)(2,1)} custom-call(s32[3]{0:T(128)} %pad_add_fusion.where_ref, bf16[1024,7168]{1,0:T(8,128)(2,1)} %gate_w_ref.1, bf16[1024,7168]{1,0:T(8,128)(2,1)} %up_w_ref.1), custom_call_target="tpu_custom_call" | custom-call | bytes 3670016 | tf_op jit(solution)/shard_map/weight_slices/pallas_call | solution.py:235
  27.9 1.5 collective-permute-start.3
  29.5 1.5 collective-permute-start.4
  30.9 1.5 collective-permute-start.5
  32.4 4.1 %pack_tokens.1 = bf16[16,256,128]{2,1,0:T(8,128)(2,1)} custom-call(s32[1]{0:T(128)} %bitcast.core_ref, bf16[128,4096]{1,0:T(8,128)(2,1)} %own_ref.1, bf16[128,4096]{1,0:T(8,128)(2,1)} %collective-permute-done.other_ref), custom_call_target="tpu_custom_call" | custom-call | bytes 3145728 | tf_op jit(solution)/shard_map/pack_tokens/pallas_call | solution.py:274
  37.2 22.4 %local_ranks.1 = (f32[2,128,512]{2,1,0:T(8,128)}, bf16[2,128,512]{2,1,0:T(8,128)(2,1)}) custom-call(s32[1]{0:T(128)} %bitcast.core_ref, bf16[2,128,512]{2,1,0:T(8,128)(2,1)} %pad_maximum_fusion.2.own_ref, bf16[2,128,512]{2,1,0:T(8,128)(2,1)} %copy-done.12, bf16[1024,7168]{1,0:T(8,128)(2,1)} %gate_w_ref.1, bf16[1024,7168]{1,0:T(8,128)(2,1)} %up_w_ref.1, ...), custom_call_target="tpu_custom_call" | custom-call | flops 7516192768 | bytes 31195136 | tf_op jit(solution)/shard_map/local_ranks/pallas_call | solution.py:184
  59.6 10.5 %collective-permute-done.3 = bf16[2,128,512]{2,1,0:T(8,128)(2,1)S(1)} collective-permute-done((bf16[2,128,512]{2,1,0:T(8,128)(2,1)}, bf16[2,128,512]{2,1,0:T(8,128)(2,1)S(1)}, u32[]{:S(2)}, u32[]{:S(2)}) %collective-permute-start.3) | collective-permute-done | bytes 262176 | tf_op jit(solution)/shard_map/ppermute | solution.py:470
  70.1 4.9 %collective-permute-done.4 = bf16[2,128,512]{2,1,0:T(8,128)(2,1)S(1)} collective-permute-done((bf16[2,128,512]{2,1,0:T(8,128)(2,1)}, bf16[2,128,512]{2,1,0:T(8,128)(2,1)S(1)}, u32[]{:S(2)}, u32[]{:S(2)}) %collective-permute-start.4) | collective-permute-done | bytes 262176 | tf_op jit(solution)/shard_map/ppermute | solution.py:470
  77.7 1.7 collective-permute-start.10
  84.0 1.8 collective-permute-start.12
  85.7 1.9 collective-permute-start.13
  87.7 12.1 %input_terms.1 = (bf16[128,4096]{1,0:T(8,128)(2,1)}, f32[128,4096]{1,0:T(8,128)}) custom-call(s32[1]{0:T(128)} %bitcast.core_ref, bf16[2,128,512]{2,1,0:T(8,128)(2,1)} %copy-done.3, bf16[8192,512]{1,0:T(8,128)(2,1)} %gate_ref.3, bf16[8192,512]{1,0:T(8,128)(2,1)} %up_ref.3), custom_call_target="tpu_custom_call" | custom-call | flops 2147483648 | bytes 19922944 | tf_op jit(solution)/shard_map/input_terms/pallas_call | solution.py:402
  99.8 4.9 %all-to-all-start = ((bf16[16,256,128]{2,1,0:T(8,128)(2,1)}), bf16[16,256,128]{2,1,0:T(8,128)(2,1)}, u32[]{:S(2)}, u32[]{:S(2)}) async-start(bf16[16,256,128]{2,1,0:T(8,128)(2,1)} %pack_tokens.1), calls=%async_computation | async-start | bytes 2097152 | tf_op jit(solution)/shard_map/all_to_all | solution.py:44
  104.7 6.8 %right_part.3.refs_4_ = f32[2,896,512]{2,1,0:T(8,128)} custom-call(s32[3]{0:T(128)} %add_add_fusion.where_ref, bf16[2,4,128,512]{3,2,1,0:T(8,128)(2,1)} %copy-done.2, bf16[2,4,128,512]{3,2,1,0:T(8,128)(2,1)} %collective-permute-done.6.refs_1_, bf16[4,4,448,128]{3,2,1,0:T(8,128)(2,1)} %bitcast.35, bf16[2,448,1024]{2,1,0:T(8,128)(2,1)} %weight_slices.1.refs_3_.refs_5_), custom_call_target="tpu_custom_call" | custom-call | flops 1879048192 | bytes 3932160 | tf_op jit(solution)/shard_map/right_part/pallas_call | solution.py:339
  111.6 3.8 %collective-permute-done.13 = bf16[2,128,512]{2,1,0:T(8,128)(2,1)} collective-permute-done((bf16[2,128,512]{2,1,0:T(8,128)(2,1)S(1)}, bf16[2,128,512]{2,1,0:T(8,128)(2,1)}, u32[]{:S(2)}, u32[]{:S(2)}) %collective-permute-start.13) | collective-permute-done | bytes 262176 | tf_op jit(solution)/shard_map/ppermute | solution.py:470
  115.3 1.9 slice_bitcast_fusion.3
  117.7 1.9 slice_bitcast_fusion.2
  125.8 2.0 collective-permute-start.15
  127.8 7.9 %right_part.4.refs_4_ = f32[2,896,512]{2,1,0:T(8,128)} custom-call(s32[3]{0:T(128)} %add_add_fusion.3.where_ref, bf16[2,4,128,512]{3,2,1,0:T(8,128)(2,1)} %collective-permute-done.9.refs_0_, bf16[2,4,128,512]{3,2,1,0:T(8,128)(2,1)} %collective-permute-done.19.refs_1_, bf16[4,4,448,128]{3,2,1,0:T(8,128)(2,1)} %bitcast.36, ...), custom_call_target="tpu_custom_call", output_to_operand_aliasing={{}: (5, {})} | custom-call | flops 1879048192 | bytes 3932160 | tf_op jit(solution)/shard_map/right_part/pallas_call | solution.py:339
  136.7 7.9 %right_part.5.refs_6_ = f32[2,896,512]{2,1,0:T(8,128)} custom-call(s32[3]{0:T(128)} %add_add_fusion.2.where_ref, bf16[2,4,128,512]{3,2,1,0:T(8,128)(2,1)} %collective-permute-done.10.refs_0_, bf16[2,4,128,512]{3,2,1,0:T(8,128)(2,1)} %copy-done.6, bf16[4,4,448,128]{3,2,1,0:T(8,128)(2,1)} %bitcast.37, ...), custom_call_target="tpu_custom_call", output_to_operand_aliasing={{}: (5, {})} | custom-call | flops 1879048192 | bytes 3932160 | tf_op jit(solution)/shard_map/right_part/pallas_call | solution.py:339
  148.2 7.4 %right_last.1 = bf16[16,64,896]{2,1,0:T(8,128)(2,1)} custom-call(s32[3]{0:T(128)} %add_add_fusion.1.where_ref, bf16[4,128,512]{2,1,0:T(8,128)(2,1)} %copy-done.8, bf16[4,128,512]{2,1,0:T(8,128)(2,1)} %copy-done.9, bf16[4,128,512]{2,1,0:T(8,128)(2,1)} %copy-done.10, bf16[4,128,512]{2,1,0:T(8,128)(2,1)} %copy-done.11, bf16[4,4,448,128]{3,2,1,0:T(8,128)(2,1)} %bitcast.38, ...), custom_call_target="tpu_custom_call" | custom-call | flops 1879048192 | bytes 3932160 | tf_op jit(solution)/shard_map/right_last/pallas_call | solution.py:339
  155.6 3.6 %collective-permute-done.14.refs_1_ = bf16[2,4,128,512]{3,2,1,0:T(8,128)(2,1)} collective-permute-done((bf16[2,4,128,512]{3,2,1,0:T(8,128)(2,1)}, bf16[2,4,128,512]{3,2,1,0:T(8,128)(2,1)}, u32[]{:S(2)}, u32[]{:S(2)}) %collective-permute-start.14) | collective-permute-done | bytes 1048608 | tf_op jit(solution)/shard_map/ppermute | solution.py:480
  159.3 5.9 %all-to-all-start.2 = ((bf16[16,64,896]{2,1,0:T(8,128)(2,1)}), bf16[16,64,896]{2,1,0:T(8,128)(2,1)S(1)}, u32[]{:S(2)}, u32[]{:S(2)}) async-start(bf16[16,64,896]{2,1,0:T(8,128)(2,1)} %right_last.1), calls=%async_computation.2 | async-start | bytes 3670016 | tf_op jit(solution)/shard_map/all_to_all | solution.py:44
  166.9 1.5 collective-permute-start.22
  171.3 21.0 %collective-permute-done.22.refs_3_ = bf16[4,128,512]{2,1,0:T(8,128)(2,1)S(1)} collective-permute-done((bf16[4,128,512]{2,1,0:T(8,128)(2,1)S(1)}, bf16[4,128,512]{2,1,0:T(8,128)(2,1)S(1)}, u32[]{:S(2)}, u32[]{:S(2)}) %collective-permute-start.22) | collective-permute-done | bytes 524320 | tf_op jit(solution)/shard_map/ppermute | solution.py:480
  193.1 5.9 %left_grads.1 = (bf16[512,512]{1,0:T(8,128)(2,1)}, bf16[512,512]{1,0:T(8,128)(2,1)}) custom-call(s32[3]{0:T(128)} %add_add_fusion.where_ref, bf16[4,4,256,128]{3,2,1,0:T(8,128)(2,1)} %bitcast.9.own, bf16[4,4,256,128]{3,2,1,0:T(8,128)(2,1)} %copy-done.15, bf16[2,4,128,512]{3,2,1,0:T(8,128)(2,1)} %pad_maximum_fusion.1.refs_0_, ...), custom_call_target="tpu_custom_call" | custom-call | flops 2147483648 | bytes 6291456 | tf_op jit(solution)/shard_map/left_grads/pallas_call | solution.py:452
  199.0 8.0 %all-to-all-done.2.in_ref = bf16[16,64,896]{2,1,0:T(8,128)(2,1)S(1)} async-done(((bf16[16,64,896]{2,1,0:T(8,128)(2,1)}), bf16[16,64,896]{2,1,0:T(8,128)(2,1)S(1)}, u32[]{:S(2)}, u32[]{:S(2)}) %all-to-all-start.2) | async-done | bytes 1835040 | tf_op jit(solution)/shard_map/all_to_all | solution.py:44
  208.3 3.2 %settle.1 = (bf16[64,7168]{1,0:T(8,128)(2,1)}, bf16[64,7168]{1,0:T(8,128)(2,1)}) custom-call(bf16[16,64,896]{2,1,0:T(8,128)(2,1)} %copy-done.1), custom_call_target="tpu_custom_call" | custom-call | bytes 3670016 | tf_op jit(solution)/shard_map/settle/pallas_call | solution.py:370
  (95 shorter events, 27.3 us)
Async XLA Ops:
  0.6 11.4 %collective-permute-start = (bf16[128,4096]{1,0:T(8,128)(2,1)}, bf16[128,4096]{1,0:T(8,128)(2,1)}, u32[]{:S(2)}, u32[]{:S(2)}) collective-permute-start(bf16[128,4096]{1,0:T(8,128)(2,1)} %own_ref.1), channel_id=1, source_target_pairs={{0,1},{1,0},{2,3},{3,2},{4,5},{5,4},{6,7},{7,6},{8,9},{9,8},{10,11... | collective-permute-start | bytes 3145736 | tf_op jit(solution)/shard_map/ppermute | solution.py:149
  4.7 95.2 %all-to-all-start.1 = ((bf16[16,448,128]{2,1,0:T(8,128)(2,1)}), bf16[16,448,128]{2,1,0:T(8,128)(2,1)S(1)}, u32[]{:S(2)}, u32[]{:S(2)}) async-start(bf16[16,448,128]{2,1,0:T(8,128)(2,1)} %bitcast.39), calls=%async_computation.1 | async-start | bytes 3670016 | tf_op jit(solution)/shard_map/all_to_all | solution.py:44
  23.5 13.0 %collective-permute-start.1 = (bf16[2,128,512]{2,1,0:T(8,128)(2,1)}, bf16[2,128,512]{2,1,0:T(8,128)(2,1)S(1)}, u32[]{:S(2)}, u32[]{:S(2)}) collective-permute-start(bf16[2,128,512]{2,1,0:T(8,128)(2,1)} %pad_maximum_fusion.2.own_ref), channel_id=1, source_target_pairs={{0,1},{1,0},{2,3},{3,2},{4,5},{5,4},{6,7},{7,6},{8,9},{9,8},{10,11... | collective-permute-start | bytes 786440 | tf_op jit(solution)/shard_map/ppermute | solution.py:149
  27.9 42.1 %collective-permute-start.3 = (bf16[2,128,512]{2,1,0:T(8,128)(2,1)}, bf16[2,128,512]{2,1,0:T(8,128)(2,1)S(1)}, u32[]{:S(2)}, u32[]{:S(2)}) collective-permute-start(bf16[2,128,512]{2,1,0:T(8,128)(2,1)} %pad_maximum_fusion.2.own_ref), channel_id=1, source_target_pairs={{0,8},{2,10},{4,12},{6,14},{8,16},{10,18},{12,20},{14,22},{16,24},... | collective-permute-start | bytes 786440 | tf_op jit(solution)/shard_map/ppermute | solution.py:470
  29.5 45.5 %collective-permute-start.4 = (bf16[2,128,512]{2,1,0:T(8,128)(2,1)}, bf16[2,128,512]{2,1,0:T(8,128)(2,1)S(1)}, u32[]{:S(2)}, u32[]{:S(2)}) collective-permute-start(bf16[2,128,512]{2,1,0:T(8,128)(2,1)} %pad_maximum_fusion.2.own_ref), channel_id=1, source_target_pairs={{0,16},{2,18},{4,20},{6,22},{8,24},{10,26},{12,28},{14,30},{16,0},... | collective-permute-start | bytes 786440 | tf_op jit(solution)/shard_map/ppermute | solution.py:470
  30.9 45.4 %collective-permute-start.5 = (bf16[2,128,512]{2,1,0:T(8,128)(2,1)}, bf16[2,128,512]{2,1,0:T(8,128)(2,1)S(1)}, u32[]{:S(2)}, u32[]{:S(2)}) collective-permute-start(bf16[2,128,512]{2,1,0:T(8,128)(2,1)} %pad_maximum_fusion.2.own_ref), channel_id=1, source_target_pairs={{0,24},{2,26},{4,28},{6,30},{8,0},{10,2},{12,4},{14,6},{16,8},{18,... | collective-permute-start | bytes 786440 | tf_op jit(solution)/shard_map/ppermute | solution.py:470
  77.6 22.2 %copy-start.2 = (bf16[2,4,128,512]{3,2,1,0:T(8,128)(2,1)}, bf16[2,4,128,512]{3,2,1,0:T(8,128)(2,1)S(1)}, u32[]{:S(2)}) copy-start(bf16[2,4,128,512]{3,2,1,0:T(8,128)(2,1)S(1)} %pad_maximum_fusion.refs_0_) | copy-start | bytes 3145732
  77.7 6.2 %collective-permute-start.6 = (bf16[2,4,128,512]{3,2,1,0:T(8,128)(2,1)S(1)}, bf16[2,4,128,512]{3,2,1,0:T(8,128)(2,1)}, u32[]{:S(2)}, u32[]{:S(2)}) collective-permute-start(bf16[2,4,128,512]{3,2,1,0:T(8,128)(2,1)S(1)} %pad_maximum_fusion.refs_0_), channel_id=1, source_target_pairs={{0,1},{1,0},{2,3},{3,2},{4,5},{5,4},{6,7},{7,6},{8,9},{9,8},{10,11... | collective-permute-start | bytes 3145736 | tf_op jit(solution)/shard_map/ppermute | solution.py:149
  77.7 33.8 %collective-permute-start.10 = (bf16[2,4,128,512]{3,2,1,0:T(8,128)(2,1)S(1)}, bf16[2,4,128,512]{3,2,1,0:T(8,128)(2,1)}, u32[]{:S(2)}, u32[]{:S(2)}) collective-permute-start(bf16[2,4,128,512]{3,2,1,0:T(8,128)(2,1)S(1)} %pad_maximum_fusion.refs_0_), channel_id=1, source_target_pairs={{0,4},{2,6},{4,0},{6,2},{8,12},{10,14},{12,8},{14,10},{16,20},{18,... | collective-permute-start | bytes 3145736 | tf_op jit(solution)/shard_map/ppermute | solution.py:480
  79.4 32.1 %collective-permute-start.9 = (bf16[2,4,128,512]{3,2,1,0:T(8,128)(2,1)S(1)}, bf16[2,4,128,512]{3,2,1,0:T(8,128)(2,1)}, u32[]{:S(2)}, u32[]{:S(2)}) collective-permute-start(bf16[2,4,128,512]{3,2,1,0:T(8,128)(2,1)S(1)} %pad_maximum_fusion.refs_0_), channel_id=1, source_target_pairs={{0,2},{2,0},{4,6},{6,4},{8,10},{10,8},{12,14},{14,12},{16,18},{18,... | collective-permute-start | bytes 3145736 | tf_op jit(solution)/shard_map/ppermute | solution.py:480
  80.9 1.9 collective-permute-start.2
  83.9 27.6 %collective-permute-start.11 = (bf16[2,128,512]{2,1,0:T(8,128)(2,1)S(1)}, bf16[2,128,512]{2,1,0:T(8,128)(2,1)S(1)}, u32[]{:S(2)}, u32[]{:S(2)}) collective-permute-start(bf16[2,128,512]{2,1,0:T(8,128)(2,1)S(1)} %add_convert_fusion.1.ranks_ref), channel_id=1, source_target_pairs={{0,8},{2,10},{4,12},{6,14},{8,16},{10,18},{12,20},{14,22},{16,24},... | collective-permute-start | bytes 786440 | tf_op jit(solution)/shard_map/ppermute | solution.py:470
  84.0 27.6 %collective-permute-start.12 = (bf16[2,128,512]{2,1,0:T(8,128)(2,1)S(1)}, bf16[2,128,512]{2,1,0:T(8,128)(2,1)}, u32[]{:S(2)}, u32[]{:S(2)}) collective-permute-start(bf16[2,128,512]{2,1,0:T(8,128)(2,1)S(1)} %add_convert_fusion.1.ranks_ref), channel_id=1, source_target_pairs={{0,16},{2,18},{4,20},{6,22},{8,24},{10,26},{12,28},{14,30},{16,0},... | collective-permute-start | bytes 786440 | tf_op jit(solution)/shard_map/ppermute | solution.py:470
  85.7 29.6 %collective-permute-start.13 = (bf16[2,128,512]{2,1,0:T(8,128)(2,1)S(1)}, bf16[2,128,512]{2,1,0:T(8,128)(2,1)}, u32[]{:S(2)}, u32[]{:S(2)}) collective-permute-start(bf16[2,128,512]{2,1,0:T(8,128)(2,1)S(1)} %add_convert_fusion.1.ranks_ref), channel_id=1, source_target_pairs={{0,24},{2,26},{4,28},{6,30},{8,0},{10,2},{12,4},{14,6},{16,8},{18,... | collective-permute-start | bytes 786440 | tf_op jit(solution)/shard_map/ppermute | solution.py:470
  99.8 59.4 %all-to-all-start = ((bf16[16,256,128]{2,1,0:T(8,128)(2,1)}), bf16[16,256,128]{2,1,0:T(8,128)(2,1)}, u32[]{:S(2)}, u32[]{:S(2)}) async-start(bf16[16,256,128]{2,1,0:T(8,128)(2,1)} %pack_tokens.1), calls=%async_computation | async-start | bytes 2097152 | tf_op jit(solution)/shard_map/all_to_all | solution.py:44
  111.5 9.5 %copy-start.4 = (bf16[2,128,512]{2,1,0:T(8,128)(2,1)S(1)}, bf16[2,128,512]{2,1,0:T(8,128)(2,1)}, u32[]{:S(2)}) copy-start(bf16[2,128,512]{2,1,0:T(8,128)(2,1)} %copy-done.3) | copy-start | bytes 786436
  111.5 8.0 %copy-start.13 = (bf16[2,128,512]{2,1,0:T(8,128)(2,1)}, bf16[2,128,512]{2,1,0:T(8,128)(2,1)S(1)}, u32[]{:S(2)}) copy-start(bf16[2,128,512]{2,1,0:T(8,128)(2,1)S(1)} %collective-permute-done.11) | copy-start | bytes 786436
  115.3 10.5 %collective-permute-start.19 = (bf16[2,4,128,512]{3,2,1,0:T(8,128)(2,1)}, bf16[2,4,128,512]{3,2,1,0:T(8,128)(2,1)}, u32[]{:S(2)}, u32[]{:S(2)}) collective-permute-start(bf16[2,4,128,512]{3,2,1,0:T(8,128)(2,1)} %collective-permute-done.9.refs_0_), channel_id=1, source_target_pairs={{0,1},{1,0},{2,3},{3,2},{4,5},{5,4},{6,7},{7,6},{8,9},{9,8},{10,11... | collective-permute-start | bytes 3145736 | tf_op jit(solution)/shard_map/ppermute | solution.py:149
  117.2 18.5 %collective-permute-start.18 = (bf16[2,4,128,512]{3,2,1,0:T(8,128)(2,1)}, bf16[2,4,128,512]{3,2,1,0:T(8,128)(2,1)S(1)}, u32[]{:S(2)}, u32[]{:S(2)}) collective-permute-start(bf16[2,4,128,512]{3,2,1,0:T(8,128)(2,1)} %collective-permute-done.10.refs_0_), channel_id=1, source_target_pairs={{0,1},{1,0},{2,3},{3,2},{4,5},{5,4},{6,7},{7,6},{8,9},{9,8},{10,11... | collective-permute-start | bytes 3145736 | tf_op jit(solution)/shard_map/ppermute | solution.py:149
  119.6 25.1 %collective-permute-start.16 = (bf16[4,128,512]{2,1,0:T(8,128)(2,1)}, bf16[4,128,512]{2,1,0:T(8,128)(2,1)S(1)}, u32[]{:S(2)}, u32[]{:S(2)}) collective-permute-start(bf16[4,128,512]{2,1,0:T(8,128)(2,1)} %slice_bitcast_fusion.3), channel_id=1, source_target_pairs={{0,4},{2,6},{4,0},{6,2},{8,12},{10,14},{12,8},{14,10},{16,20},{18,... | collective-permute-start | bytes 1572872 | tf_op jit(solution)/shard_map/ppermute | solution.py:480
  119.6 25.1 %collective-permute-start.17 = (bf16[4,128,512]{2,1,0:T(8,128)(2,1)}, bf16[4,128,512]{2,1,0:T(8,128)(2,1)S(1)}, u32[]{:S(2)}, u32[]{:S(2)}) collective-permute-start(bf16[4,128,512]{2,1,0:T(8,128)(2,1)} %slice_bitcast_fusion.2), channel_id=1, source_target_pairs={{0,2},{2,0},{4,6},{6,4},{8,10},{10,8},{12,14},{14,12},{16,18},{18,... | collective-permute-start | bytes 1572872 | tf_op jit(solution)/shard_map/ppermute | solution.py:480
  125.2 34.0 %collective-permute-start.14 = (bf16[2,4,128,512]{3,2,1,0:T(8,128)(2,1)}, bf16[2,4,128,512]{3,2,1,0:T(8,128)(2,1)}, u32[]{:S(2)}, u32[]{:S(2)}) collective-permute-start(bf16[2,4,128,512]{3,2,1,0:T(8,128)(2,1)} %pad_maximum_fusion.1.refs_0_), channel_id=1, source_target_pairs={{0,2},{2,0},{4,6},{6,4},{8,10},{10,8},{12,14},{14,12},{16,18},{18,... | collective-permute-start | bytes 3145736 | tf_op jit(solution)/shard_map/ppermute | solution.py:480
  125.8 33.5 %collective-permute-start.15 = (bf16[2,4,128,512]{3,2,1,0:T(8,128)(2,1)}, bf16[2,4,128,512]{3,2,1,0:T(8,128)(2,1)}, u32[]{:S(2)}, u32[]{:S(2)}) collective-permute-start(bf16[2,4,128,512]{3,2,1,0:T(8,128)(2,1)} %pad_maximum_fusion.1.refs_0_), channel_id=1, source_target_pairs={{0,4},{2,6},{4,0},{6,2},{8,12},{10,14},{12,8},{14,10},{16,20},{18,... | collective-permute-start | bytes 3145736 | tf_op jit(solution)/shard_map/ppermute | solution.py:480
  144.6 2.0 collective-permute-start.20
  144.7 2.6 %collective-permute-start.21 = (bf16[4,128,512]{2,1,0:T(8,128)(2,1)S(1)}, bf16[4,128,512]{2,1,0:T(8,128)(2,1)S(1)}, u32[]{:S(2)}, u32[]{:S(2)}) collective-permute-start(bf16[4,128,512]{2,1,0:T(8,128)(2,1)S(1)} %collective-permute-done.17.refs_1_), channel_id=1, source_target_pairs={{0,1},{1,0},{2,3},{3,2},{4,5},{5,4},{6,7},{7,6},{8,9},{9,8},{10,11... | collective-permute-start | bytes 1572872 | tf_op jit(solution)/shard_map/ppermute | solution.py:149
  155.6 9.6 %copy-start.14 = (bf16[128,4096]{1,0:T(8,128)(2,1)S(1)}, bf16[128,4096]{1,0:T(8,128)(2,1)}, u32[]{:S(2)}) copy-start(bf16[128,4096]{1,0:T(8,128)(2,1)} %get-tuple-element.43) | copy-start | bytes 3145732
  159.3 47.8 %all-to-all-start.2 = ((bf16[16,64,896]{2,1,0:T(8,128)(2,1)}), bf16[16,64,896]{2,1,0:T(8,128)(2,1)S(1)}, u32[]{:S(2)}, u32[]{:S(2)}) async-start(bf16[16,64,896]{2,1,0:T(8,128)(2,1)} %right_last.1), calls=%async_computation.2 | async-start | bytes 3670016 | tf_op jit(solution)/shard_map/all_to_all | solution.py:44
  165.2 4.9 %collective-permute-start.7 = (bf16[128,4096]{1,0:T(8,128)(2,1)S(1)}, bf16[128,4096]{1,0:T(8,128)(2,1)S(1)}, u32[]{:S(2)}, u32[]{:S(2)}) collective-permute-start(bf16[128,4096]{1,0:T(8,128)(2,1)S(1)} %copy-done.14), channel_id=1, source_target_pairs={{0,1},{1,0},{2,3},{3,2},{4,5},{5,4},{6,7},{7,6},{8,9},{9,8},{10,11... | collective-permute-start | bytes 3145736 | tf_op jit(solution)/shard_map/ppermute | solution.py:149
  165.3 6.0 %collective-permute-start.8 = (bf16[4,4,256,128]{3,2,1,0:T(8,128)(2,1)}, bf16[4,4,256,128]{3,2,1,0:T(8,128)(2,1)S(1)}, u32[]{:S(2)}, u32[]{:S(2)}) collective-permute-start(bf16[4,4,256,128]{3,2,1,0:T(8,128)(2,1)} %bitcast.9.own), channel_id=1, source_target_pairs={{0,1},{1,0},{2,3},{3,2},{4,5},{5,4},{6,7},{7,6},{8,9},{9,8},{10,11... | collective-permute-start | bytes 3145736 | tf_op jit(solution)/shard_map/ppermute | solution.py:149
  166.9 25.4 %collective-permute-start.22 = (bf16[4,128,512]{2,1,0:T(8,128)(2,1)S(1)}, bf16[4,128,512]{2,1,0:T(8,128)(2,1)S(1)}, u32[]{:S(2)}, u32[]{:S(2)}) collective-permute-start(bf16[4,128,512]{2,1,0:T(8,128)(2,1)S(1)} %slice_bitcast_fusion.1), channel_id=1, source_target_pairs={{0,4},{2,6},{4,0},{6,2},{8,12},{10,14},{12,8},{14,10},{16,20},{18,... | collective-permute-start | bytes 1572872 | tf_op jit(solution)/shard_map/ppermute | solution.py:480
  169.5 22.8 %collective-permute-start.23 = (bf16[4,128,512]{2,1,0:T(8,128)(2,1)S(1)}, bf16[4,128,512]{2,1,0:T(8,128)(2,1)}, u32[]{:S(2)}, u32[]{:S(2)}) collective-permute-start(bf16[4,128,512]{2,1,0:T(8,128)(2,1)S(1)} %slice_bitcast_fusion), channel_id=1, source_target_pairs={{0,2},{2,0},{4,6},{6,4},{8,10},{10,8},{12,14},{14,12},{16,18},{18,... | collective-permute-start | bytes 1572872 | tf_op jit(solution)/shard_map/ppermute | solution.py:480
  171.3 21.0 %copy-start.15 = (bf16[4,4,256,128]{3,2,1,0:T(8,128)(2,1)}, bf16[4,4,256,128]{3,2,1,0:T(8,128)(2,1)S(1)}, u32[]{:S(2)}) copy-start(bf16[4,4,256,128]{3,2,1,0:T(8,128)(2,1)S(1)} %collective-permute-done.8.other) | copy-start | bytes 3145732
  (13 other events, 35.3 us)
